TPU v7x, 32 devices: a whole 2x2x4 slice. The times are simulated.
32 devices in a mesh: groups: 2 (over y), ctx: 4 (over z), head: 2 (over x), qsub: 2 (over core).
Axes of the slice: x: 2, y: 2, z: 4, core: 2. Of those that a mesh axis runs over, the one named last changes fastest.
Arguments:
- queries: bfloat16 [4096, 2, 8, 128], P(('groups', 'ctx'), 'head', 'qsub'), parts along dimension 0, may hold values from -7 to 7
- key_states: bfloat16 [4096, 2, 128], P(('groups', 'ctx'), 'head'), parts along dimension 0, may hold values from -4 to 4
- value_states: bfloat16 [4096, 2, 128], P(('groups', 'ctx'), 'head'), parts along dimension 0, may hold values from -6 to 6
- block_table: int32 [16, 7], P(('groups', 'ctx')), parts along dimension 0, may hold values from -1 to 6, as said below
Outputs:
- attended: bfloat16 [4096, 2, 8, 128], P(('groups', 'ctx'), 'head', 'qsub'), parts along dimension 0
There are 2 independent parts, one for each index of `groups`. A program takes and returns all parts, laid end to end along the dimension named above; each array names one. Nothing has to cross between parts.
Inputs may be any that keep to these rules, and one draw needn't show every extreme that they name: `block_table`: entry [b, k] is -1 or b - 2 ** k, and never below 0; it is b - 2 ** k wherever that value is 0 or 1, and in column 0 wherever b >= 1.
All inputs are finite; a program needn't handle non-finite values.
Results may differ from a plain program's by a relative error of at most 0.0044.
Values may be sent and summed in bfloat16 or wider, within the bound.
No kernel may reach another device: no remote copies, remote signals or barrier semaphores. Data moves between devices by JAX's collectives and lax.ppermute only.
A program may use at most 64 MiB of HBM per device.

v0:
```python
import functools
import math
from functools import reduce

import jax
import jax.numpy as jnp
from jax import lax
from jax.experimental import pallas as pl
from jax.experimental.pallas import tpu as pltpu
from jax.sharding import PartitionSpec as P

DH = 128
BLOCK = 256
SINKS = 4
LEVELS = 7
TILE = 512
NEG = -1e30
BIG = 1e30
EXP2_SCALE = DH ** (-0.5) * math.log2(math.e)
ONES = 16


def named(table_ref, i, u):
    return reduce(lambda a, b: a | b, [table_ref[i, level] == u for level in range(LEVELS)])


def counts_of(kind, table_ref, i, block, u, first_here, blocks_here):
    before = (u >= 0) & (u < block)
    elsewhere = (u < first_here) | (u >= first_here + blocks_here)
    if kind == "all":
        return before & elsewhere & ((u < SINKS) | named(table_ref, i, u))
    if kind == "sink":
        return before & elsewhere & (u < SINKS)
    return before & elsewhere & (u >= SINKS) & named(table_ref, i, u)


def scores(k, q):
    return lax.dot_general(k, q, (((1,), (1,)), ((), ())), preferred_element_type=jnp.float32)


def widened(v, vt_ref):
    vt_ref[:DH, :] = v.T
    vt_ref[DH:, :] = jnp.ones((ONES, v.shape[0]), v.dtype)


def combine(q, items, before):
    raw, tops = [], [] if before is None else [before]
    for k, _, counts, mask in items:
        s = scores(k, q)
        if mask is not None:
            s = jnp.where(mask, s, NEG)
        top = jnp.max(s, axis=0, keepdims=True)
        raw.append(s)
        tops.append(top if counts is None else jnp.where(counts, top, NEG))
    highest = reduce(jnp.maximum, tops)
    scaled = highest * EXP2_SCALE
    total = None
    for s, (_, vt, counts, _) in zip(raw, items):
        shift = scaled if counts is None else jnp.where(counts, scaled, BIG)
        w = jnp.exp2(s * EXP2_SCALE - shift).astype(jnp.bfloat16)
        part = jnp.dot(vt, w, preferred_element_type=jnp.float32)
        total = part if total is None else total + part
    return total, highest


def keep_state(acc_ref, stat_ref, cols, acc, highest, total):
    acc_ref[:, cols] = acc
    stat_ref[:8, cols] = jnp.broadcast_to(highest, (8, TILE))
    stat_ref[8:, cols] = jnp.broadcast_to(total, (8, TILE))


def local_stage(per_head, cores, q_ref, *refs):
    refs = list(refs)
    parts = [refs.pop(0) for _ in range(cores)]
    table_ref = refs.pop(0) if len(refs) == 6 else None
    acc_ref, stat_ref, k_ref, v_ref, vt_ref = refs
    core = lax.axis_index("qsub")
    part = parts[0].shape[1]
    for shift, ref in enumerate(parts):
        at = pl.ds(pl.multiple_of(lax.rem(core - shift + cores, cores) * part, part), part)
        k_ref[at, :] = ref[0]
        v_ref[at, :] = ref[1]
    blocks_here = k_ref.shape[0] // BLOCK
    rows_per_block = BLOCK * per_head
    widened(v_ref[...], vt_ref)
    first_here = lax.axis_index("ctx") * blocks_here
    tokens = TILE // per_head
    for i in range(blocks_here):
        for t in range(rows_per_block // TILE):
            cols = pl.ds(i * rows_per_block + t * TILE, TILE)
            items = []
            for j in range(i):
                span = pl.ds(j * BLOCK, BLOCK)
                u = first_here + j
                counts = None if j == i - 1 else (u < SINKS) | named(table_ref, i, u)
                items.append((k_ref[span, :], vt_ref[:, span], counts, None))
            if t:
                span = pl.ds(i * BLOCK, t * tokens)
                items.append((k_ref[span, :], vt_ref[:, span], None, None))
            span = pl.ds(i * BLOCK + t * tokens, tokens)
            token = lax.broadcasted_iota(jnp.int32, (tokens, TILE), 1) // per_head
            mask = lax.broadcasted_iota(jnp.int32, (tokens, TILE), 0) <= token
            items.append((k_ref[span, :], vt_ref[:, span], None, mask))
            sums, highest = combine(q_ref[cols, :], items, None)
            keep_state(acc_ref, stat_ref, cols, sums[:DH], highest, sums[DH : DH + 8])


def arrival_stage(pieces, blocks_here, last, table_ref, q_ref, acc_in, stat_in, *refs):
    refs = list(refs)
    arrived = [refs.pop(0) for _ in pieces]
    if last:
        out_hbm, out_ref, vt_ref, sems = refs
    else:
        acc_ref, stat_ref, vt_ref = refs
    me, core = lax.axis_index("ctx"), lax.axis_index("qsub")
    first_here = me * blocks_here
    rows_per_block = q_ref.shape[0] // blocks_here
    blocks = []
    for (kind, base, count), ref in zip(pieces, arrived):
        start = base(me, core)
        for j in range(count):
            span = pl.ds(j * BLOCK, BLOCK)
            at = len(blocks)
            blocks.append((ref.at[0, span, :], vt_ref.at[at], kind, jnp.where(start < 0, -1, start + j), ref.at[1, span, :]))
    counts = [
        [counts_of(kind, table_ref, i, first_here + i, u, first_here, blocks_here) for _, _, kind, u, _ in blocks]
        for i in range(blocks_here)
    ]
    some = [reduce(lambda a, b: a | b, row) for row in counts]

    @pl.when(reduce(lambda a, b: a | b, some))
    def _():
        for _, vt, _, _, values in blocks:
            widened(values[...], vt)

    copies = []

    def finish(cols, acc, highest, total):
        if last:
            out_ref[cols, :] = (acc / total[:1]).astype(out_ref.dtype).T
        else:
            keep_state(acc_ref, stat_ref, cols, acc, highest, total)

    for i in range(blocks_here):
        tiles = [pl.ds(i * rows_per_block + t * TILE, TILE) for t in range(rows_per_block // TILE)]

        @pl.when(some[i])
        def _():
            for cols in tiles:
                items = [(k[...], vt[...], c, None) for (k, vt, _, _, _), c in zip(blocks, counts[i])]
                before = stat_in[:1, cols]
                sums, highest = combine(q_ref[cols, :], items, before)
                keep = jnp.exp2((before - highest) * EXP2_SCALE)
                finish(cols, acc_in[:, cols] * keep + sums[:DH], highest, stat_in[8:, cols] * keep + sums[DH : DH + 8])

        @pl.when(jnp.logical_not(some[i]))
        def _():
            for cols in tiles:
                finish(cols, acc_in[:, cols], stat_in[:1, cols], stat_in[8:, cols])

        if last:
            rows = pl.ds(i * rows_per_block, rows_per_block)
            copy = pltpu.make_async_copy(out_ref.at[rows], out_hbm.at[rows], sems.at[i])
            copy.start()
            copies.append(copy)
    for copy in copies:
        copy.wait()


VMEM_SPEC = pl.BlockSpec(memory_space=pltpu.VMEM)
ANY_SPEC = pl.BlockSpec(memory_space=pl.ANY)
PARAMS = pltpu.CompilerParams(vmem_limit_bytes=16 << 20)


def state_shapes(rows):
    return [jax.ShapeDtypeStruct((DH, rows), jnp.float32), jax.ShapeDtypeStruct((16, rows), jnp.float32)]


def cost(rows, keys):
    return pl.CostEstimate(flops=4 * rows * keys * DH, bytes_accessed=8 * rows * DH, transcendentals=rows * keys)


def call_local(q, parts, table, per_head):
    rows, tokens = q.shape[0], sum(a.shape[1] for a in parts)
    needs_table = tokens // BLOCK > 2
    return pl.pallas_call(
        functools.partial(local_stage, per_head, len(parts)),
        in_specs=[VMEM_SPEC] * (1 + len(parts)) + [pl.BlockSpec(memory_space=pltpu.SMEM)] * needs_table,
        out_specs=[VMEM_SPEC] * 2,
        out_shape=state_shapes(rows),
        scratch_shapes=[
            pltpu.VMEM((tokens, DH), q.dtype),
            pltpu.VMEM((tokens, DH), q.dtype),
            pltpu.VMEM((DH + ONES, tokens), q.dtype),
        ],
        cost_estimate=cost(rows, BLOCK),
        compiler_params=PARAMS,
        name="local",
    )(*([q, *parts] + [table] * needs_table))


def call_arrival(pieces, arrays, table, q, state, last, blocks_here, name):
    rows = q.shape[0]
    keys = sum(a.shape[1] for a in arrays)
    scratch = [pltpu.VMEM((keys // BLOCK, DH + ONES, BLOCK), q.dtype)]
    if last:
        scratch = [pltpu.VMEM(q.shape, q.dtype), *scratch, pltpu.SemaphoreType.DMA((blocks_here,))]
    return pl.pallas_call(
        functools.partial(arrival_stage, pieces, blocks_here, last),
        in_specs=[pl.BlockSpec(memory_space=pltpu.SMEM)] + [VMEM_SPEC] * (3 + len(arrays)),
        out_specs=ANY_SPEC if last else [VMEM_SPEC] * 2,
        out_shape=jax.ShapeDtypeStruct(q.shape, q.dtype) if last else state_shapes(rows),
        scratch_shapes=scratch,
        cost_estimate=cost(rows, keys),
        compiler_params=PARAMS,
        name=name,
    )(table, q, *state, *arrays)


def shards(queries, key_states, value_states, block_table):
    tokens = queries.shape[0]
    per_head = queries.shape[2]
    blocks_here = tokens // BLOCK
    context_count = lax.axis_size("ctx")
    cores = lax.axis_size("qsub")
    per_core = blocks_here // cores
    core = lax.axis_index("qsub")
    q = queries.reshape(tokens * per_head, DH)
    k = key_states.reshape(tokens, DH)
    v = value_states.reshape(tokens, DH)
    run = functools.partial(call_arrival, table=block_table, q=q, blocks_here=blocks_here)

    part = per_core * BLOCK
    packed = jnp.stack(
        [lax.dynamic_slice_in_dim(k, core * part, part), lax.dynamic_slice_in_dim(v, core * part, part)]
    )

    def swapped(arrived):
        return [arrived] + [
            lax.ppermute(arrived, "qsub", [(c, (c + shift) % cores) for c in range(cores)]) for shift in range(1, cores)
        ]

    def both_cores(arrived, kind, source):
        pieces = []
        for shift in range(cores):
            base = lambda me, core, shift=shift: jnp.where(
                source(me) < 0, -1, source(me) * blocks_here + lax.rem(core - shift + cores, cores) * per_core
            )
            pieces.append((kind, base, per_core))
        return pieces, swapped(arrived)

    if context_count == 4:
        ring = [0, 1, 3, 2]
        after = {d: ring[(ring.index(d) + 1) % 4] for d in ring}
        before = {d: ring[(ring.index(d) - 1) % 4] for d in ring}
        look = lambda pairs: lambda me: reduce(
            lambda acc, d: jnp.where(me == d, pairs[d], acc), range(4), jnp.int32(0)
        )
        forward = [(d, after[d]) for d in range(4)]
        backward = [(d, before[d]) for d in range(4)]
        one = lax.ppermute(packed, "ctx", backward)
        state = call_local(q, swapped(packed), block_table, per_head)
        held, one, state = lax.optimization_barrier((packed, one, state))
        other = lax.ppermute(held, "ctx", forward)
        two = lax.ppermute(one, "ctx", backward)
        arrivals = [
            (one, look(after)),
            (other, look(before)),
            (two, look({d: after[after[d]] for d in range(4)})),
        ]
        for n, (arrived, source) in enumerate(arrivals):
            if n:
                arrived = later[n - 1]
            pieces, arrays = both_cores(arrived, "all", source)
            state = run(pieces, arrays, state=state, last=n == 2, name=f"arrival_{n}")
            if n == 0:
                other, state = lax.optimization_barrier((other, state))
                two, state = lax.optimization_barrier((two, state))
                later = (other, two)
        attended = state
    else:
        state = call_local(q, swapped(packed), block_table, per_head)
        wanted = []
        for level in range(LEVELS):
            amount = max(2**level // blocks_here, 1)
            if amount < context_count and amount not in wanted:
                wanted.append(amount)
        roots = -(-SINKS // blocks_here)
        position = lax.axis_index("ctx")
        shared = [
            lax.psum(jnp.where(position == root, packed, jnp.zeros_like(packed)), "ctx") for root in range(roots)
        ]
        source_of = packed
        reached = 0
        stages = []
        for amount in wanted:
            hop = amount - reached
            source_of = lax.ppermute(source_of, "ctx", [(d, d + hop) for d in range(context_count - hop)])
            reached = amount
            stages.append(both_cores(source_of, "level", lambda me, amount=amount: jnp.maximum(me - amount, -1)))
        for root, arrived in enumerate(shared):
            stages.append(both_cores(arrived, "sink", lambda me, root=root: jnp.int32(root)))
        for n, (pieces, arrays) in enumerate(stages):
            state = run(pieces, arrays, state=state, last=n == len(stages) - 1, name=f"arrival_{n}")
        attended = state
    return attended.reshape(tokens, 1, per_head, DH)


def solution(mesh):
    placed = (
        P(("groups", "ctx"), "head", "qsub", None),
        P(("groups", "ctx"), "head", None),
        P(("groups", "ctx"), "head", None),
        P(("groups", "ctx"), None),
    )
    return jax.shard_map(
        shards,
        mesh=mesh,
        in_specs=placed,
        out_specs=P(("groups", "ctx"), "head", "qsub", None),
        check_vma=False,
    )
```

profile of v0, /device:TPU:31, one launch (start us, length us, event | category | flops | bytes accessed | tf_op | source)
XLA Modules:
  0.0 26.2 jit_solution(10631977527285208470)
XLA Ops:
  0.0 0.0 copy-start
  0.0 0.9 %dynamic-slice_bitcast_fusion = (bf16[1,256,128]{2,1,0:T(8,128)(2,1)S(1)}, bf16[1,256,128]{2,1,0:T(8,128)(2,1)S(1)}) fusion(bf16[512,1,128]{2,0,1:T(8,128)(2,1)} %param.6, s32[]{:T(128)S(6)} %select_n.4, bf16[512,1,128]{2,0,1:T(8,128)(2,1)} %param.5), kind=kLoop, calls=%fused_computation.1 | loop fusion | bytes 262148 | tf_op jit(solution)/shard_map/stack | solution.py:234
  1.0 0.7 %collective-permute-start.1 = (bf16[2,256,128]{2,1,0:T(8,128)(2,1)S(1)}, bf16[2,256,128]{2,1,0:T(8,128)(2,1)S(1)}, u32[]{:S(2)}, u32[]{:S(2)}) collective-permute-start(bf16[2,256,128]{2,1,0:T(8,128)(2,1)S(1)} %pad_maximum_fusion.refs_0_), channel_id=1, source_target_pairs={{0,1},{1,0},{2,3},{3,2},{4,5},{5,4},{6,7},{7,6},{8,9},{9,8},{10,11... | collective-permute-start | bytes 393224 | tf_op jit(solution)/shard_map/ppermute | solution.py:240
  1.7 0.1 collective-permute-start
  1.8 0.9 %collective-permute-done.1.refs_1_ = bf16[2,256,128]{2,1,0:T(8,128)(2,1)S(1)} collective-permute-done((bf16[2,256,128]{2,1,0:T(8,128)(2,1)S(1)}, bf16[2,256,128]{2,1,0:T(8,128)(2,1)S(1)}, u32[]{:S(2)}, u32[]{:S(2)}) %collective-permute-start.1) | collective-permute-done | bytes 131104 | tf_op jit(solution)/shard_map/ppermute | solution.py:240
  2.7 0.0 copy-done
  2.7 1.8 %local.1 = (f32[128,2048]{1,0:T(8,128)S(1)}, f32[16,2048]{1,0:T(8,128)S(1)}) custom-call(bf16[2048,128]{1,0:T(8,128)(2,1)S(1)} %bitcast.8, bf16[2,256,128]{2,1,0:T(8,128)(2,1)S(1)} %pad_maximum_fusion.refs_0_, bf16[2,256,128]{2,1,0:T(8,128)(2,1)S(1)} %collective-permute-done.1.refs_1_), custom_call_target="tpu_custom_call" | custom-call | flops 268435456 | bytes 2097152 | tf_op jit(solution)/shard_map/local/pallas_call | solution.py:186
  4.5 2.2 %collective-permute-done.refs_0_ = bf16[2,256,128]{2,1,0:T(8,128)(2,1)S(1)} collective-permute-done((bf16[2,256,128]{2,1,0:T(8,128)(2,1)S(1)}, bf16[2,256,128]{2,1,0:T(8,128)(2,1)S(1)}, u32[]{:S(2)}, u32[]{:S(2)}) %collective-permute-start) | collective-permute-done | bytes 131104 | tf_op jit(solution)/shard_map/ppermute | solution.py:261
  6.7 0.0 copy-start.1
  6.7 0.9 %collective-permute-start.4 = (bf16[2,256,128]{2,1,0:T(8,128)(2,1)S(1)}, bf16[2,256,128]{2,1,0:T(8,128)(2,1)S(1)}, u32[]{:S(2)}, u32[]{:S(2)}) collective-permute-start(bf16[2,256,128]{2,1,0:T(8,128)(2,1)S(1)} %collective-permute-done.refs_0_), channel_id=1, source_target_pairs={{0,1},{1,0},{2,3},{3,2},{4,5},{5,4},{6,7},{7,6},{8,9},{9,8},{10,11... | collective-permute-start | bytes 393224 | tf_op jit(solution)/shard_map/ppermute | solution.py:240
  7.6 1.1 %collective-permute-start.3 = (bf16[2,256,128]{2,1,0:T(8,128)(2,1)S(1)}, bf16[2,256,128]{2,1,0:T(8,128)(2,1)S(1)}, u32[]{:S(2)}, u32[]{:S(2)}) collective-permute-start(bf16[2,256,128]{2,1,0:T(8,128)(2,1)S(1)} %pad_maximum_fusion.refs_0_), channel_id=1, source_target_pairs={{0,4},{4,12},{8,0},{12,8},{1,5},{5,13},{9,1},{13,9},{2,6},{6,14},{... | collective-permute-start | bytes 393224 | tf_op jit(solution)/shard_map/ppermute | solution.py:264
  8.7 1.3 %collective-permute-start.2 = (bf16[2,256,128]{2,1,0:T(8,128)(2,1)S(1)}, bf16[2,256,128]{2,1,0:T(8,128)(2,1)S(1)}, u32[]{:S(2)}, u32[]{:S(2)}) collective-permute-start(bf16[2,256,128]{2,1,0:T(8,128)(2,1)S(1)} %collective-permute-done.refs_0_), channel_id=1, source_target_pairs={{0,8},{4,0},{8,12},{12,4},{1,9},{5,1},{9,13},{13,5},{2,10},{6,2},{... | collective-permute-start | bytes 393224 | tf_op jit(solution)/shard_map/ppermute | solution.py:265
  10.0 0.0 collective-permute-done.4.refs_1_
  10.0 0.0 copy-done.1
  10.0 2.1 %arrival_0.1 = (f32[128,2048]{1,0:T(8,128)S(1)}, f32[16,2048]{1,0:T(8,128)S(1)}) custom-call(s32[2,7]{1,0:T(2,128)S(1)} %copy-done.1, bf16[2048,128]{1,0:T(8,128)(2,1)S(1)} %bitcast.9, f32[128,2048]{1,0:T(8,128)S(1)} %get-tuple-element.25.acc_in, f32[16,2048]{1,0:T(8,128)S(1)} %get-tuple-element.26.stat_in, ...), custom_call_target="tpu_custom_call" | custom-call | flops 536870912 | bytes 2097152 | tf_op jit(solution)/shard_map/arrival_0/pallas_call | solution.py:208
  12.1 1.7 %collective-permute-done.3.refs_0_ = bf16[2,256,128]{2,1,0:T(8,128)(2,1)S(1)} collective-permute-done((bf16[2,256,128]{2,1,0:T(8,128)(2,1)S(1)}, bf16[2,256,128]{2,1,0:T(8,128)(2,1)S(1)}, u32[]{:S(2)}, u32[]{:S(2)}) %collective-permute-start.3) | collective-permute-done | bytes 131104 | tf_op jit(solution)/shard_map/ppermute | solution.py:264
  13.9 3.4 %collective-permute-start.5 = (bf16[2,256,128]{2,1,0:T(8,128)(2,1)S(1)}, bf16[2,256,128]{2,1,0:T(8,128)(2,1)S(1)}, u32[]{:S(2)}, u32[]{:S(2)}) collective-permute-start(bf16[2,256,128]{2,1,0:T(8,128)(2,1)S(1)} %collective-permute-done.3.refs_0_), channel_id=1, source_target_pairs={{0,1},{1,0},{2,3},{3,2},{4,5},{5,4},{6,7},{7,6},{8,9},{9,8},{10,11... | collective-permute-start | bytes 393224 | tf_op jit(solution)/shard_map/ppermute | solution.py:240
  17.3 0.0 collective-permute-done.2.refs_0_
  17.3 0.0 collective-permute-start.6
  17.3 1.0 %collective-permute-done.5.refs_1_ = bf16[2,256,128]{2,1,0:T(8,128)(2,1)S(1)} collective-permute-done((bf16[2,256,128]{2,1,0:T(8,128)(2,1)S(1)}, bf16[2,256,128]{2,1,0:T(8,128)(2,1)S(1)}, u32[]{:S(2)}, u32[]{:S(2)}) %collective-permute-start.5) | collective-permute-done | bytes 131104 | tf_op jit(solution)/shard_map/ppermute | solution.py:240
  18.3 3.5 %arrival_1.1 = (f32[128,2048]{1,0:T(8,128)S(1)}, f32[16,2048]{1,0:T(8,128)S(1)}) custom-call(s32[2,7]{1,0:T(2,128)S(1)} %copy-done.1, bf16[2048,128]{1,0:T(8,128)(2,1)S(1)} %bitcast.10, f32[128,2048]{1,0:T(8,128)S(1)} %get-tuple-element.31.acc_in, f32[16,2048]{1,0:T(8,128)S(1)} %get-tuple-element.32.stat_in, ...), custom_call_target="tpu_custom_call" | custom-call | flops 536870912 | bytes 2097152 | tf_op jit(solution)/shard_map/arrival_1/pallas_call | solution.py:208
  21.8 0.0 collective-permute-done.6.refs_1_
  21.8 4.4 %arrival_2.1 = bf16[2048,128]{1,0:T(8,128)(2,1)} custom-call(s32[2,7]{1,0:T(2,128)S(1)} %copy-done.1, bf16[2048,128]{1,0:T(8,128)(2,1)S(1)} %bitcast.11, f32[128,2048]{1,0:T(8,128)S(1)} %get-tuple-element.34.acc_in, f32[16,2048]{1,0:T(8,128)S(1)} %get-tuple-element.35.stat_in, bf16[2,256,128]{2,1,0:T(8,128)(2,1)S(1)} %collective-permute-done.2.refs_0_, ...), custom_call_target="tpu_custom_call" | custom-call | flops 536870912 | bytes 2097152 | tf_op jit(solution)/shard_map/arrival_2/pallas_call | solution.py:208
  (1 shorter events, 0.0 us)
Async XLA Ops:
  0.0 2.7 %copy-start = (bf16[512,1,4,128]{3,2,1,0:T(4,128)(2,1)S(1)}, bf16[512,1,4,128]{3,2,1,0:T(4,128)(2,1)}, u32[]{:S(2)}) copy-start(bf16[512,1,4,128]{3,2,1,0:T(4,128)(2,1)} %param.4) | copy-start | bytes 1572868
  1.0 1.7 %collective-permute-start.1 = (bf16[2,256,128]{2,1,0:T(8,128)(2,1)S(1)}, bf16[2,256,128]{2,1,0:T(8,128)(2,1)S(1)}, u32[]{:S(2)}, u32[]{:S(2)}) collective-permute-start(bf16[2,256,128]{2,1,0:T(8,128)(2,1)S(1)} %pad_maximum_fusion.refs_0_), channel_id=1, source_target_pairs={{0,1},{1,0},{2,3},{3,2},{4,5},{5,4},{6,7},{7,6},{8,9},{9,8},{10,11... | collective-permute-start | bytes 393224 | tf_op jit(solution)/shard_map/ppermute | solution.py:240
  1.7 5.0 %collective-permute-start = (bf16[2,256,128]{2,1,0:T(8,128)(2,1)S(1)}, bf16[2,256,128]{2,1,0:T(8,128)(2,1)S(1)}, u32[]{:S(2)}, u32[]{:S(2)}) collective-permute-start(bf16[2,256,128]{2,1,0:T(8,128)(2,1)S(1)} %pad_maximum_fusion.refs_0_), channel_id=1, source_target_pairs={{0,8},{4,0},{8,12},{12,4},{1,9},{5,1},{9,13},{13,5},{2,10},{6,2},{... | collective-permute-start | bytes 393224 | tf_op jit(solution)/shard_map/ppermute | solution.py:261
  6.7 3.3 %copy-start.1 = (s32[2,7]{1,0:T(2,128)S(1)}, s32[2,7]{1,0:T(2,128)}, u32[]{:S(2)}) copy-start(s32[2,7]{1,0:T(2,128)} %table_ref.5) | copy-start | bytes 172
  6.7 3.3 %collective-permute-start.4 = (bf16[2,256,128]{2,1,0:T(8,128)(2,1)S(1)}, bf16[2,256,128]{2,1,0:T(8,128)(2,1)S(1)}, u32[]{:S(2)}, u32[]{:S(2)}) collective-permute-start(bf16[2,256,128]{2,1,0:T(8,128)(2,1)S(1)} %collective-permute-done.refs_0_), channel_id=1, source_target_pairs={{0,1},{1,0},{2,3},{3,2},{4,5},{5,4},{6,7},{7,6},{8,9},{9,8},{10,11... | collective-permute-start | bytes 393224 | tf_op jit(solution)/shard_map/ppermute | solution.py:240
  7.6 6.3 %collective-permute-start.3 = (bf16[2,256,128]{2,1,0:T(8,128)(2,1)S(1)}, bf16[2,256,128]{2,1,0:T(8,128)(2,1)S(1)}, u32[]{:S(2)}, u32[]{:S(2)}) collective-permute-start(bf16[2,256,128]{2,1,0:T(8,128)(2,1)S(1)} %pad_maximum_fusion.refs_0_), channel_id=1, source_target_pairs={{0,4},{4,12},{8,0},{12,8},{1,5},{5,13},{9,1},{13,9},{2,6},{6,14},{... | collective-permute-start | bytes 393224 | tf_op jit(solution)/shard_map/ppermute | solution.py:264
  8.7 8.6 %collective-permute-start.2 = (bf16[2,256,128]{2,1,0:T(8,128)(2,1)S(1)}, bf16[2,256,128]{2,1,0:T(8,128)(2,1)S(1)}, u32[]{:S(2)}, u32[]{:S(2)}) collective-permute-start(bf16[2,256,128]{2,1,0:T(8,128)(2,1)S(1)} %collective-permute-done.refs_0_), channel_id=1, source_target_pairs={{0,8},{4,0},{8,12},{12,4},{1,9},{5,1},{9,13},{13,5},{2,10},{6,2},{... | collective-permute-start | bytes 393224 | tf_op jit(solution)/shard_map/ppermute | solution.py:265
  13.9 4.4 %collective-permute-start.5 = (bf16[2,256,128]{2,1,0:T(8,128)(2,1)S(1)}, bf16[2,256,128]{2,1,0:T(8,128)(2,1)S(1)}, u32[]{:S(2)}, u32[]{:S(2)}) collective-permute-start(bf16[2,256,128]{2,1,0:T(8,128)(2,1)S(1)} %collective-permute-done.3.refs_0_), channel_id=1, source_target_pairs={{0,1},{1,0},{2,3},{3,2},{4,5},{5,4},{6,7},{7,6},{8,9},{9,8},{10,11... | collective-permute-start | bytes 393224 | tf_op jit(solution)/shard_map/ppermute | solution.py:240
  17.3 4.5 %collective-permute-start.6 = (bf16[2,256,128]{2,1,0:T(8,128)(2,1)S(1)}, bf16[2,256,128]{2,1,0:T(8,128)(2,1)S(1)}, u32[]{:S(2)}, u32[]{:S(2)}) collective-permute-start(bf16[2,256,128]{2,1,0:T(8,128)(2,1)S(1)} %collective-permute-done.2.refs_0_), channel_id=1, source_target_pairs={{0,1},{1,0},{2,3},{3,2},{4,5},{5,4},{6,7},{7,6},{8,9},{9,8},{10,11... | collective-permute-start | bytes 393224 | tf_op jit(solution)/shard_map/ppermute | solution.py:240
where the time goes:
time: 26.4 us; the launch traced here: 26.2 us
  Pallas kernels  11.8 us (45%)
  starting transfers between devices  7.49 us (28%)
  waiting for transfers between devices  5.87 us (22%)
  local copies, waits for them, and re-layouts  0.95 us (4%)
    pallas_call x3, Pallas kernels, call_arrival(): pl.pallas_call(functools.partial(arrival_stage, pieces, blocks_here, last...  10.1 us
    ppermute x4, starting transfers between devices, swapped(): lax.ppermute(arrived, 'qsub', [(c, (c + shift) % cores) for c in range(co...  5.07 us
    ppermute x1, waiting for transfers between devices, shards(): one = lax.ppermute(packed, 'ctx', backward)  2.22 us
    ppermute x4, waiting for transfers between devices, swapped(): lax.ppermute(arrived, 'qsub', [(c, (c + shift) % cores) for c in range(co...  1.91 us
    pallas_call x1, Pallas kernels, call_local(): pl.pallas_call(functools.partial(local_stage, per_head, len(parts)), in_s...  1.78 us
    ppermute x1, waiting for transfers between devices, shards(): other = lax.ppermute(held, 'ctx', forward)  1.74 us
    ppermute x1, starting transfers between devices, shards(): two = lax.ppermute(one, 'ctx', backward)  1.3 us
    ppermute x1, starting transfers between devices, shards(): other = lax.ppermute(held, 'ctx', forward)  1.07 us
  transfers between devices with their start and end apart: 7, of which 4 were waited for; matrix products, arithmetic and copies ran while one was open for 0% of the time, Pallas kernels for 28%

commit v1 on v0

--- a/solution.py
+++ b/solution.py
@@ -8,6 +8,7 @@
 from jax.experimental import pallas as pl
 from jax.experimental.pallas import tpu as pltpu
 from jax.sharding import PartitionSpec as P
+
 
 DH = 128
 BLOCK = 256
@@ -105,66 +106,79 @@
             keep_state(acc_ref, stat_ref, cols, sums[:DH], highest, sums[DH : DH + 8])
 
 
-def arrival_stage(pieces, blocks_here, last, table_ref, q_ref, acc_in, stat_in, *refs):
-    refs = list(refs)
-    arrived = [refs.pop(0) for _ in pieces]
-    if last:
-        out_hbm, out_ref, vt_ref, sems = refs
-    else:
-        acc_ref, stat_ref, vt_ref = refs
+def flags_stage(stages, blocks_here, table_ref, flags_ref):
     me, core = lax.axis_index("ctx"), lax.axis_index("qsub")
     first_here = me * blocks_here
+    for n, pieces in enumerate(stages):
+        at = 0
+        for kind, base, count in pieces:
+            start = base(me, core)
+            for j in range(count):
+                u = jnp.where(start < 0, -1, start + j)
+                for i in range(blocks_here):
+                    counts = counts_of(kind, table_ref, i, first_here + i, u, first_here, blocks_here)
+                    flags_ref[n, at] = counts.astype(jnp.int32)
+                    at += 1
+
+
+def arrival_stage(stage, operands, blocks_here, last, flags_ref, q_ref, acc_in, stat_in, *refs):
+    refs = list(refs)
+    arrived = [refs.pop(0) for _ in range(operands)]
+    if last:
+        out_hbm, out_ref, k_ref, vt_ref, sems = refs
+    else:
+        acc_ref, stat_ref, k_ref, vt_ref = refs
     rows_per_block = q_ref.shape[0] // blocks_here
-    blocks = []
-    for (kind, base, count), ref in zip(pieces, arrived):
-        start = base(me, core)
-        for j in range(count):
-            span = pl.ds(j * BLOCK, BLOCK)
-            at = len(blocks)
-            blocks.append((ref.at[0, span, :], vt_ref.at[at], kind, jnp.where(start < 0, -1, start + j), ref.at[1, span, :]))
-    counts = [
-        [counts_of(kind, table_ref, i, first_here + i, u, first_here, blocks_here) for _, _, kind, u, _ in blocks]
-        for i in range(blocks_here)
-    ]
-    some = [reduce(lambda a, b: a | b, row) for row in counts]
-
-    @pl.when(reduce(lambda a, b: a | b, some))
+    tiles = q_ref.shape[0] // TILE
+    key_blocks = k_ref.shape[0] // BLOCK
+    counts = [[flags_ref[stage, j * blocks_here + i] > 0 for j in range(key_blocks)] for i in range(blocks_here)]
+    some = reduce(lambda a, b: a | b, sum(counts, []))
+
+    def finish(t, acc, highest, total):
+        cols = pl.ds(t * TILE, TILE)
+        if not last:
+            keep_state(acc_ref, stat_ref, cols, acc, highest, total)
+            return
+        out_ref[cols, :] = (acc / total[:1]).astype(out_ref.dtype).T
+        pltpu.make_async_copy(out_ref.at[cols], out_hbm.at[cols], sems.at[t]).start()
+
+    @pl.when(some)
     def _():
-        for _, vt, _, _, values in blocks:
-            widened(values[...], vt)
-
-    copies = []
-
-    def finish(cols, acc, highest, total):
-        if last:
-            out_ref[cols, :] = (acc / total[:1]).astype(out_ref.dtype).T
-        else:
-            keep_state(acc_ref, stat_ref, cols, acc, highest, total)
-
-    for i in range(blocks_here):
-        tiles = [pl.ds(i * rows_per_block + t * TILE, TILE) for t in range(rows_per_block // TILE)]
-
-        @pl.when(some[i])
-        def _():
-            for cols in tiles:
-                items = [(k[...], vt[...], c, None) for (k, vt, _, _, _), c in zip(blocks, counts[i])]
-                before = stat_in[:1, cols]
-                sums, highest = combine(q_ref[cols, :], items, before)
-                keep = jnp.exp2((before - highest) * EXP2_SCALE)
-                finish(cols, acc_in[:, cols] * keep + sums[:DH], highest, stat_in[8:, cols] * keep + sums[DH : DH + 8])
-
-        @pl.when(jnp.logical_not(some[i]))
-        def _():
-            for cols in tiles:
-                finish(cols, acc_in[:, cols], stat_in[:1, cols], stat_in[8:, cols])
-
-        if last:
-            rows = pl.ds(i * rows_per_block, rows_per_block)
-            copy = pltpu.make_async_copy(out_ref.at[rows], out_hbm.at[rows], sems.at[i])
-            copy.start()
-            copies.append(copy)
-    for copy in copies:
-        copy.wait()
+        at = 0
+        for ref in arrived:
+            span = pl.ds(at, ref.shape[1])
+            k_ref[span, :] = ref[0]
+            vt_ref[:DH, span] = ref[1].T
+            at += ref.shape[1]
+        vt_ref[DH:, :] = jnp.ones((ONES, at), vt_ref.dtype)
+        k, vt = k_ref[...], vt_ref[...]
+        raw = scores(k, q_ref[pl.ds(0, TILE), :])
+        for t in range(tiles):
+            s = raw
+            if t + 1 < tiles:
+                raw = scores(k, q_ref[pl.ds((t + 1) * TILE, TILE), :])
+            cols = pl.ds(t * TILE, TILE)
+            row = counts[t * TILE // rows_per_block]
+            parts = [s[j * BLOCK : (j + 1) * BLOCK] for j in range(len(row))]
+            tops = [jnp.where(c, jnp.max(part, axis=0, keepdims=True), NEG) for c, part in zip(row, parts)]
+            before = stat_in[:1, cols]
+            highest = reduce(jnp.maximum, tops, before)
+            scaled = highest * EXP2_SCALE
+            w = [jnp.exp2(part * EXP2_SCALE - jnp.where(c, scaled, BIG)).astype(vt.dtype) for c, part in zip(row, parts)]
+            sums = jnp.dot(vt, jnp.concatenate(w, axis=0), preferred_element_type=jnp.float32)
+            keep = jnp.exp2((before - highest) * EXP2_SCALE)
+            finish(t, acc_in[:, cols] * keep + sums[:DH], highest, stat_in[8:, cols] * keep + sums[DH : DH + 8])
+
+    @pl.when(jnp.logical_not(some))
+    def _():
+        for t in range(tiles):
+            cols = pl.ds(t * TILE, TILE)
+            finish(t, acc_in[:, cols], stat_in[:1, cols], stat_in[8:, cols])
+
+    if last:
+        for t in range(tiles):
+            rows = pl.ds(t * TILE, TILE)
+            pltpu.make_async_copy(out_ref.at[rows], out_hbm.at[rows], sems.at[t]).wait()
 
 
 VMEM_SPEC = pl.BlockSpec(memory_space=pltpu.VMEM)
@@ -199,22 +213,33 @@
     )(*([q, *parts] + [table] * needs_table))
 
 
-def call_arrival(pieces, arrays, table, q, state, last, blocks_here, name):
+def call_flags(stages, table, blocks_here):
+    entries = max(sum(count for _, _, count in pieces) for pieces in stages) * blocks_here
+    return pl.pallas_call(
+        functools.partial(flags_stage, stages, blocks_here),
+        in_specs=[pl.BlockSpec(memory_space=pltpu.SMEM)],
+        out_specs=pl.BlockSpec(memory_space=pltpu.SMEM),
+        out_shape=jax.ShapeDtypeStruct((len(stages), entries), jnp.int32),
+        compiler_params=PARAMS,
+        name="flags",
+    )(table)
+
+
+def call_arrival(stage, arrays, flags, q, state, last, blocks_here):
     rows = q.shape[0]
     keys = sum(a.shape[1] for a in arrays)
-    scratch = [pltpu.VMEM((keys // BLOCK, DH + ONES, BLOCK), q.dtype)]
+    scratch = [pltpu.VMEM((keys, DH), q.dtype), pltpu.VMEM((DH + ONES, keys), q.dtype)]
     if last:
-        scratch = [pltpu.VMEM(q.shape, q.dtype), *scratch, pltpu.SemaphoreType.DMA((blocks_here,))]
+        scratch = [pltpu.VMEM(q.shape, q.dtype), *scratch, pltpu.SemaphoreType.DMA((rows // TILE,))]
     return pl.pallas_call(
-        functools.partial(arrival_stage, pieces, blocks_here, last),
+        functools.partial(arrival_stage, stage, len(arrays), blocks_here, last),
         in_specs=[pl.BlockSpec(memory_space=pltpu.SMEM)] + [VMEM_SPEC] * (3 + len(arrays)),
         out_specs=ANY_SPEC if last else [VMEM_SPEC] * 2,
         out_shape=jax.ShapeDtypeStruct(q.shape, q.dtype) if last else state_shapes(rows),
         scratch_shapes=scratch,
         cost_estimate=cost(rows, keys),
         compiler_params=PARAMS,
-        name=name,
-    )(table, q, *state, *arrays)
+    )(flags, q, *state, *arrays)
 
 
 def shards(queries, key_states, value_states, block_table):
@@ -228,7 +253,7 @@
     q = queries.reshape(tokens * per_head, DH)
     k = key_states.reshape(tokens, DH)
     v = value_states.reshape(tokens, DH)
-    run = functools.partial(call_arrival, table=block_table, q=q, blocks_here=blocks_here)
+    run = functools.partial(call_arrival, q=q, blocks_here=blocks_here)
 
     part = per_core * BLOCK
     packed = jnp.stack(
@@ -240,14 +265,14 @@
             lax.ppermute(arrived, "qsub", [(c, (c + shift) % cores) for c in range(cores)]) for shift in range(1, cores)
         ]
 
-    def both_cores(arrived, kind, source):
+    def pieces_of(kind, source):
         pieces = []
         for shift in range(cores):
             base = lambda me, core, shift=shift: jnp.where(
                 source(me) < 0, -1, source(me) * blocks_here + lax.rem(core - shift + cores, cores) * per_core
             )
             pieces.append((kind, base, per_core))
-        return pieces, swapped(arrived)
+        return pieces
 
     if context_count == 4:
         ring = [0, 1, 3, 2]
@@ -260,23 +285,20 @@
         backward = [(d, before[d]) for d in range(4)]
         one = lax.ppermute(packed, "ctx", backward)
         state = call_local(q, swapped(packed), block_table, per_head)
-        held, one, state = lax.optimization_barrier((packed, one, state))
+        held, state = lax.optimization_barrier((packed, state))
+        one, state = lax.optimization_barrier((one, state))
         other = lax.ppermute(held, "ctx", forward)
         two = lax.ppermute(one, "ctx", backward)
-        arrivals = [
-            (one, look(after)),
-            (other, look(before)),
-            (two, look({d: after[after[d]] for d in range(4)})),
-        ]
-        for n, (arrived, source) in enumerate(arrivals):
-            if n:
-                arrived = later[n - 1]
-            pieces, arrays = both_cores(arrived, "all", source)
-            state = run(pieces, arrays, state=state, last=n == 2, name=f"arrival_{n}")
+        sources = [look(after), look(before), look({d: after[after[d]] for d in range(4)})]
+        flags = call_flags([pieces_of("all", source) for source in sources], block_table, blocks_here)
+        arrivals = [one, other, two]
+        for n in range(3):
+            arrays = swapped(arrivals[n])
+            state = run(n, arrays, flags, state=state, last=n == 2)
             if n == 0:
                 other, state = lax.optimization_barrier((other, state))
                 two, state = lax.optimization_barrier((two, state))
-                later = (other, two)
+                arrivals = [one, other, two]
         attended = state
     else:
         state = call_local(q, swapped(packed), block_table, per_head)
@@ -297,11 +319,12 @@
             hop = amount - reached
             source_of = lax.ppermute(source_of, "ctx", [(d, d + hop) for d in range(context_count - hop)])
             reached = amount
-            stages.append(both_cores(source_of, "level", lambda me, amount=amount: jnp.maximum(me - amount, -1)))
+            stages.append((source_of, pieces_of("level", lambda me, amount=amount: jnp.maximum(me - amount, -1))))
         for root, arrived in enumerate(shared):
-            stages.append(both_cores(arrived, "sink", lambda me, root=root: jnp.int32(root)))
-        for n, (pieces, arrays) in enumerate(stages):
-            state = run(pieces, arrays, state=state, last=n == len(stages) - 1, name=f"arrival_{n}")
+            stages.append((arrived, pieces_of("sink", lambda me, root=root: jnp.int32(root))))
+        flags = call_flags([pieces for _, pieces in stages], block_table, blocks_here)
+        for n, (arrived, _) in enumerate(stages):
+            state = run(n, swapped(arrived), flags, state=state, last=n == len(stages) - 1)
         attended = state
     return attended.reshape(tokens, 1, per_head, DH)
 
@@ -313,6 +336,7 @@
         P(("groups", "ctx"), "head", None),
         P(("groups", "ctx"), None),
     )
+
     return jax.shard_map(
         shards,
         mesh=mesh,

time: 26.4 us -> 24.4 us (0.924)
  the two profiles are of different devices: /device:TPU:31 before, /device:TPU:25 now
where the time goes in v1:
time: 24.4 us; the launch traced here: 24.3 us
  Pallas kernels  11.7 us (48%)
  starting transfers between devices  7.46 us (31%)
  waiting for transfers between devices  4.11 us (17%)
  local copies, waits for them, and re-layouts  0.95 us (4%)
    pallas_call x3, Pallas kernels, call_arrival(): pl.pallas_call(functools.partial(arrival_stage, stage, len(arrays), block...  8.59 us
    ppermute x4, starting transfers between devices, swapped(): lax.ppermute(arrived, 'qsub', [(c, (c + shift) % cores) for c in range(co...  5.04 us
    ppermute x1, waiting for transfers between devices, shards(): one = lax.ppermute(packed, 'ctx', backward)  2.19 us
    ppermute x4, waiting for transfers between devices, swapped(): lax.ppermute(arrived, 'qsub', [(c, (c + shift) % cores) for c in range(co...  1.91 us
    pallas_call x1, Pallas kernels, call_local(): pl.pallas_call(functools.partial(local_stage, per_head, len(parts)), in_s...  1.79 us
    ppermute x1, starting transfers between devices, shards(): two = lax.ppermute(one, 'ctx', backward)  1.3 us
    pallas_call x1, Pallas kernels, call_flags(): pl.pallas_call(functools.partial(flags_stage, stages, blocks_here), in_sp...  1.29 us
    ppermute x1, starting transfers between devices, shards(): other = lax.ppermute(held, 'ctx', forward)  1.07 us
  transfers between devices with their start and end apart: 7, of which 3 were waited for; matrix products, arithmetic and copies ran while one was open for 0% of the time, Pallas kernels for 34%

profile of v1, /device:TPU:25, one launch (start us, length us, event | category | flops | bytes accessed | tf_op | source)
XLA Modules:
  0.0 24.3 jit_solution(16058184066014631862)
XLA Ops:
  0.0 0.0 copy-start
  0.0 0.9 %dynamic-slice_bitcast_fusion = (bf16[1,256,128]{2,1,0:T(8,128)(2,1)S(1)}, bf16[1,256,128]{2,1,0:T(8,128)(2,1)S(1)}) fusion(bf16[512,1,128]{2,0,1:T(8,128)(2,1)} %param.6, s32[]{:T(128)S(6)} %select_n.4, bf16[512,1,128]{2,0,1:T(8,128)(2,1)} %param.5), kind=kLoop, calls=%fused_computation.1 | loop fusion | bytes 262148 | tf_op jit(solution)/shard_map/stack | solution.py:259
  1.0 0.7 %collective-permute-start.1 = (bf16[2,256,128]{2,1,0:T(8,128)(2,1)S(1)}, bf16[2,256,128]{2,1,0:T(8,128)(2,1)S(1)}, u32[]{:S(2)}, u32[]{:S(2)}) collective-permute-start(bf16[2,256,128]{2,1,0:T(8,128)(2,1)S(1)} %pad_maximum_fusion.refs_0_), channel_id=1, source_target_pairs={{0,1},{1,0},{2,3},{3,2},{4,5},{5,4},{6,7},{7,6},{8,9},{9,8},{10,11... | collective-permute-start | bytes 393224 | tf_op jit(solution)/shard_map/ppermute | solution.py:265
  1.7 0.1 collective-permute-start
  1.8 0.9 %collective-permute-done.1.refs_1_ = bf16[2,256,128]{2,1,0:T(8,128)(2,1)S(1)} collective-permute-done((bf16[2,256,128]{2,1,0:T(8,128)(2,1)S(1)}, bf16[2,256,128]{2,1,0:T(8,128)(2,1)S(1)}, u32[]{:S(2)}, u32[]{:S(2)}) %collective-permute-start.1) | collective-permute-done | bytes 131104 | tf_op jit(solution)/shard_map/ppermute | solution.py:265
  2.7 0.0 copy-done
  2.7 1.8 %local.1 = (f32[128,2048]{1,0:T(8,128)S(1)}, f32[16,2048]{1,0:T(8,128)S(1)}) custom-call(bf16[2048,128]{1,0:T(8,128)(2,1)S(1)} %bitcast.8, bf16[2,256,128]{2,1,0:T(8,128)(2,1)S(1)} %pad_maximum_fusion.refs_0_, bf16[2,256,128]{2,1,0:T(8,128)(2,1)S(1)} %collective-permute-done.1.refs_1_), custom_call_target="tpu_custom_call" | custom-call | flops 268435456 | bytes 2097152 | tf_op jit(solution)/shard_map/local/pallas_call | solution.py:200
  4.5 0.0 copy-start.1
  4.5 2.2 %collective-permute-done.refs_0_ = bf16[2,256,128]{2,1,0:T(8,128)(2,1)S(1)} collective-permute-done((bf16[2,256,128]{2,1,0:T(8,128)(2,1)S(1)}, bf16[2,256,128]{2,1,0:T(8,128)(2,1)S(1)}, u32[]{:S(2)}, u32[]{:S(2)}) %collective-permute-start) | collective-permute-done | bytes 131104 | tf_op jit(solution)/shard_map/ppermute | solution.py:286
  6.7 0.9 %collective-permute-start.4 = (bf16[2,256,128]{2,1,0:T(8,128)(2,1)S(1)}, bf16[2,256,128]{2,1,0:T(8,128)(2,1)S(1)}, u32[]{:S(2)}, u32[]{:S(2)}) collective-permute-start(bf16[2,256,128]{2,1,0:T(8,128)(2,1)S(1)} %collective-permute-done.refs_0_), channel_id=1, source_target_pairs={{0,1},{1,0},{2,3},{3,2},{4,5},{5,4},{6,7},{7,6},{8,9},{9,8},{10,11... | collective-permute-start | bytes 393224 | tf_op jit(solution)/shard_map/ppermute | solution.py:265
  7.6 1.1 %collective-permute-start.3 = (bf16[2,256,128]{2,1,0:T(8,128)(2,1)S(1)}, bf16[2,256,128]{2,1,0:T(8,128)(2,1)S(1)}, u32[]{:S(2)}, u32[]{:S(2)}) collective-permute-start(bf16[2,256,128]{2,1,0:T(8,128)(2,1)S(1)} %pad_maximum_fusion.refs_0_), channel_id=1, source_target_pairs={{0,4},{4,12},{8,0},{12,8},{1,5},{5,13},{9,1},{13,9},{2,6},{6,14},{... | collective-permute-start | bytes 393224 | tf_op jit(solution)/shard_map/ppermute | solution.py:290
  8.7 1.3 %collective-permute-start.2 = (bf16[2,256,128]{2,1,0:T(8,128)(2,1)S(1)}, bf16[2,256,128]{2,1,0:T(8,128)(2,1)S(1)}, u32[]{:S(2)}, u32[]{:S(2)}) collective-permute-start(bf16[2,256,128]{2,1,0:T(8,128)(2,1)S(1)} %collective-permute-done.refs_0_), channel_id=1, source_target_pairs={{0,8},{4,0},{8,12},{12,4},{1,9},{5,1},{9,13},{13,5},{2,10},{6,2},{... | collective-permute-start | bytes 393224 | tf_op jit(solution)/shard_map/ppermute | solution.py:291
  10.0 0.0 copy-done.1
  10.0 1.3 %flags.1.flags_ref = s32[3,4]{1,0:T(4,128)S(1)} custom-call(s32[2,7]{1,0:T(2,128)S(1)} %copy-done.1), custom_call_target="tpu_custom_call" | custom-call | tf_op jit(solution)/shard_map/flags/pallas_call | solution.py:218
  11.3 0.0 collective-permute-done.4.refs_1_
  11.3 2.6 %shard_map.46 = (f32[128,2048]{1,0:T(8,128)S(1)}, f32[16,2048]{1,0:T(8,128)S(1)}) custom-call(s32[3,4]{1,0:T(4,128)S(1)} %flags.1.flags_ref, bf16[2048,128]{1,0:T(8,128)(2,1)S(1)} %bitcast.9, f32[128,2048]{1,0:T(8,128)S(1)} %get-tuple-element.29.acc_in, f32[16,2048]{1,0:T(8,128)S(1)} %get-tuple-element.30.stat_in, ...), custom_call_target="tpu_custom_call" | custom-call | flops 536870912 | bytes 2097152 | tf_op jit(solution)/shard_map/pallas_call | solution.py:234
  13.9 0.0 collective-permute-done.3.refs_0_
  13.9 3.4 %collective-permute-start.5 = (bf16[2,256,128]{2,1,0:T(8,128)(2,1)S(1)}, bf16[2,256,128]{2,1,0:T(8,128)(2,1)S(1)}, u32[]{:S(2)}, u32[]{:S(2)}) collective-permute-start(bf16[2,256,128]{2,1,0:T(8,128)(2,1)S(1)} %collective-permute-done.3.refs_0_), channel_id=1, source_target_pairs={{0,1},{1,0},{2,3},{3,2},{4,5},{5,4},{6,7},{7,6},{8,9},{9,8},{10,11... | collective-permute-start | bytes 393224 | tf_op jit(solution)/shard_map/ppermute | solution.py:265
  17.3 0.0 collective-permute-done.2.refs_0_
  17.3 0.0 collective-permute-start.6
  17.3 1.0 %collective-permute-done.5.refs_1_ = bf16[2,256,128]{2,1,0:T(8,128)(2,1)S(1)} collective-permute-done((bf16[2,256,128]{2,1,0:T(8,128)(2,1)S(1)}, bf16[2,256,128]{2,1,0:T(8,128)(2,1)S(1)}, u32[]{:S(2)}, u32[]{:S(2)}) %collective-permute-start.5) | collective-permute-done | bytes 131104 | tf_op jit(solution)/shard_map/ppermute | solution.py:265
  18.3 2.6 %shard_map.47 = (f32[128,2048]{1,0:T(8,128)S(1)}, f32[16,2048]{1,0:T(8,128)S(1)}) custom-call(s32[3,4]{1,0:T(4,128)S(1)} %flags.1.flags_ref, bf16[2048,128]{1,0:T(8,128)(2,1)S(1)} %bitcast.10, f32[128,2048]{1,0:T(8,128)S(1)} %get-tuple-element.35.acc_in, f32[16,2048]{1,0:T(8,128)S(1)} %get-tuple-element.36.stat_in, ...), custom_call_target="tpu_custom_call" | custom-call | flops 536870912 | bytes 2097152 | tf_op jit(solution)/shard_map/pallas_call | solution.py:234
  20.9 0.0 collective-permute-done.6.refs_1_
  20.9 3.4 %shard_map.48 = bf16[2048,128]{1,0:T(8,128)(2,1)} custom-call(s32[3,4]{1,0:T(4,128)S(1)} %flags.1.flags_ref, bf16[2048,128]{1,0:T(8,128)(2,1)S(1)} %bitcast.11, f32[128,2048]{1,0:T(8,128)S(1)} %get-tuple-element.38.acc_in, f32[16,2048]{1,0:T(8,128)S(1)} %get-tuple-element.39.stat_in, bf16[2,256,128]{2,1,0:T(8,128)(2,1)S(1)} %collective-permute-done.2.refs_0_, ...), custom_call_target="tpu_custom_call" | custom-call | flops 536870912 | bytes 2097152 | tf_op jit(solution)/shard_map/pallas_call | solution.py:234
  (1 shorter events, 0.0 us)
Async XLA Ops:
  0.0 2.7 %copy-start = (bf16[512,1,4,128]{3,2,1,0:T(4,128)(2,1)S(1)}, bf16[512,1,4,128]{3,2,1,0:T(4,128)(2,1)}, u32[]{:S(2)}) copy-start(bf16[512,1,4,128]{3,2,1,0:T(4,128)(2,1)} %param.4) | copy-start | bytes 1572868
  1.0 1.7 %collective-permute-start.1 = (bf16[2,256,128]{2,1,0:T(8,128)(2,1)S(1)}, bf16[2,256,128]{2,1,0:T(8,128)(2,1)S(1)}, u32[]{:S(2)}, u32[]{:S(2)}) collective-permute-start(bf16[2,256,128]{2,1,0:T(8,128)(2,1)S(1)} %pad_maximum_fusion.refs_0_), channel_id=1, source_target_pairs={{0,1},{1,0},{2,3},{3,2},{4,5},{5,4},{6,7},{7,6},{8,9},{9,8},{10,11... | collective-permute-start | bytes 393224 | tf_op jit(solution)/shard_map/ppermute | solution.py:265
  1.7 5.0 %collective-permute-start = (bf16[2,256,128]{2,1,0:T(8,128)(2,1)S(1)}, bf16[2,256,128]{2,1,0:T(8,128)(2,1)S(1)}, u32[]{:S(2)}, u32[]{:S(2)}) collective-permute-start(bf16[2,256,128]{2,1,0:T(8,128)(2,1)S(1)} %pad_maximum_fusion.refs_0_), channel_id=1, source_target_pairs={{0,8},{4,0},{8,12},{12,4},{1,9},{5,1},{9,13},{13,5},{2,10},{6,2},{... | collective-permute-start | bytes 393224 | tf_op jit(solution)/shard_map/ppermute | solution.py:286
  4.5 5.5 %copy-start.1 = (s32[2,7]{1,0:T(2,128)S(1)}, s32[2,7]{1,0:T(2,128)}, u32[]{:S(2)}) copy-start(s32[2,7]{1,0:T(2,128)} %table_ref.1) | copy-start | bytes 172
  6.7 4.6 %collective-permute-start.4 = (bf16[2,256,128]{2,1,0:T(8,128)(2,1)S(1)}, bf16[2,256,128]{2,1,0:T(8,128)(2,1)S(1)}, u32[]{:S(2)}, u32[]{:S(2)}) collective-permute-start(bf16[2,256,128]{2,1,0:T(8,128)(2,1)S(1)} %collective-permute-done.refs_0_), channel_id=1, source_target_pairs={{0,1},{1,0},{2,3},{3,2},{4,5},{5,4},{6,7},{7,6},{8,9},{9,8},{10,11... | collective-permute-start | bytes 393224 | tf_op jit(solution)/shard_map/ppermute | solution.py:265
  7.6 6.3 %collective-permute-start.3 = (bf16[2,256,128]{2,1,0:T(8,128)(2,1)S(1)}, bf16[2,256,128]{2,1,0:T(8,128)(2,1)S(1)}, u32[]{:S(2)}, u32[]{:S(2)}) collective-permute-start(bf16[2,256,128]{2,1,0:T(8,128)(2,1)S(1)} %pad_maximum_fusion.refs_0_), channel_id=1, source_target_pairs={{0,4},{4,12},{8,0},{12,8},{1,5},{5,13},{9,1},{13,9},{2,6},{6,14},{... | collective-permute-start | bytes 393224 | tf_op jit(solution)/shard_map/ppermute | solution.py:290
  8.7 8.6 %collective-permute-start.2 = (bf16[2,256,128]{2,1,0:T(8,128)(2,1)S(1)}, bf16[2,256,128]{2,1,0:T(8,128)(2,1)S(1)}, u32[]{:S(2)}, u32[]{:S(2)}) collective-permute-start(bf16[2,256,128]{2,1,0:T(8,128)(2,1)S(1)} %collective-permute-done.refs_0_), channel_id=1, source_target_pairs={{0,8},{4,0},{8,12},{12,4},{1,9},{5,1},{9,13},{13,5},{2,10},{6,2},{... | collective-permute-start | bytes 393224 | tf_op jit(solution)/shard_map/ppermute | solution.py:291
  13.9 4.4 %collective-permute-start.5 = (bf16[2,256,128]{2,1,0:T(8,128)(2,1)S(1)}, bf16[2,256,128]{2,1,0:T(8,128)(2,1)S(1)}, u32[]{:S(2)}, u32[]{:S(2)}) collective-permute-start(bf16[2,256,128]{2,1,0:T(8,128)(2,1)S(1)} %collective-permute-done.3.refs_0_), channel_id=1, source_target_pairs={{0,1},{1,0},{2,3},{3,2},{4,5},{5,4},{6,7},{7,6},{8,9},{9,8},{10,11... | collective-permute-start | bytes 393224 | tf_op jit(solution)/shard_map/ppermute | solution.py:265
  17.3 3.6 %collective-permute-start.6 = (bf16[2,256,128]{2,1,0:T(8,128)(2,1)S(1)}, bf16[2,256,128]{2,1,0:T(8,128)(2,1)S(1)}, u32[]{:S(2)}, u32[]{:S(2)}) collective-permute-start(bf16[2,256,128]{2,1,0:T(8,128)(2,1)S(1)} %collective-permute-done.2.refs_0_), channel_id=1, source_target_pairs={{0,1},{1,0},{2,3},{3,2},{4,5},{5,4},{6,7},{7,6},{8,9},{9,8},{10,11... | collective-permute-start | bytes 393224 | tf_op jit(solution)/shard_map/ppermute | solution.py:265

commit v2 on v1

v2 whole, which is shorter than its diff:
```python
import functools
import math
from functools import reduce

import jax
import jax.numpy as jnp
from jax import lax
from jax.experimental import pallas as pl
from jax.experimental.pallas import tpu as pltpu
from jax.sharding import PartitionSpec as P


DH = 128
BLOCK = 256
SINKS = 4
LEVELS = 7
TILE = 512
NEG = -1e30
BIG = 1e30
EXP2_SCALE = DH ** (-0.5) * math.log2(math.e)
ONES = 16


def named(table_ref, i, u):
    return reduce(lambda a, b: a | b, [table_ref[i, level] == u for level in range(LEVELS)])


def counts_of(kind, table_ref, i, block, u, first_here, blocks_here):
    before = (u >= 0) & (u < block)
    elsewhere = (u < first_here) | (u >= first_here + blocks_here)
    if kind == "all":
        return before & elsewhere & ((u < SINKS) | named(table_ref, i, u))
    if kind == "sink":
        return before & elsewhere & (u < SINKS)
    return before & elsewhere & (u >= SINKS) & named(table_ref, i, u)


def scores(k, q):
    return lax.dot_general(k, q, (((1,), (1,)), ((), ())), preferred_element_type=jnp.float32)


def top_of(s):
    return jnp.max(s, axis=0, keepdims=True)


def weights(s, shift):
    return jnp.exp2(s * EXP2_SCALE - shift).astype(jnp.bfloat16)


def keep_state(acc_ref, stat_ref, cols, acc, highest, total):
    acc_ref[:, cols] = acc
    stat_ref[:8, cols] = jnp.broadcast_to(highest, (8, TILE))
    stat_ref[8:, cols] = total


def local_stage(i, per_head, cores, q_ref, *refs):
    refs = list(refs)
    parts = [refs.pop(0) for _ in range(cores)]
    table_ref = refs.pop(0) if len(refs) == 6 else None
    acc_ref, stat_ref, k_ref, v_ref, vt_ref = refs
    core = lax.axis_index("qsub")
    part = parts[0].shape[1]
    for shift, ref in enumerate(parts):
        at = pl.ds(pl.multiple_of(lax.rem(core - shift + cores, cores) * part, part), part)
        k_ref[at, :] = ref[0]
        v_ref[at, :] = ref[1]
    keys = (i + 1) * BLOCK
    vt_ref[:DH, :] = v_ref[:keys, :].T
    vt_ref[DH:, :] = jnp.ones((ONES, keys), vt_ref.dtype)
    rows_per_block = BLOCK * per_head
    tokens = TILE // per_head
    first_here = lax.axis_index("ctx") * (k_ref.shape[0] // BLOCK)
    for t in range(rows_per_block // TILE):
        q = q_ref[pl.ds(i * rows_per_block + t * TILE, TILE), :]
        edge = i * BLOCK + t * tokens
        items = []
        for j in range(i):
            s = scores(k_ref[pl.ds(j * BLOCK, BLOCK), :], q)
            if j < i - 1:
                u = first_here + j
                s = jnp.where((u < SINKS) | named(table_ref, i, u), s, NEG)
            items.append(s)
        if t:
            items.append(scores(k_ref[pl.ds(i * BLOCK, t * tokens), :], q))
        token = lax.broadcasted_iota(jnp.int32, (tokens, TILE), 1) // per_head
        mask = lax.broadcasted_iota(jnp.int32, (tokens, TILE), 0) <= token
        items.append(jnp.where(mask, scores(k_ref[pl.ds(edge, tokens), :], q), NEG))
        highest = reduce(jnp.maximum, [top_of(s) for s in items])
        w = jnp.concatenate([weights(s, highest * EXP2_SCALE) for s in items], axis=0)
        sums = jnp.dot(vt_ref[:, : edge + tokens], w, preferred_element_type=jnp.float32)
        keep_state(acc_ref, stat_ref, pl.ds(t * TILE, TILE), sums[:DH], highest, sums[DH : DH + 8])


def flags_stage(stages, blocks_here, table_ref, flags_ref):
    me, core = lax.axis_index("ctx"), lax.axis_index("qsub")
    first_here = me * blocks_here
    at = 0
    for pieces in stages:
        for kind, base, count in pieces:
            start = base(me, core)
            for j in range(count):
                u = jnp.where(start < 0, -1, start + j)
                for i in range(blocks_here):
                    counts = counts_of(kind, table_ref, i, first_here + i, u, first_here, blocks_here)
                    flags_ref[at : at + 1, :] = jnp.full((1, TILE), jnp.where(counts, 0.0, BIG), jnp.float32)
                    at += 1


def arrival_stage(source, row_of, operands, blocks_here, last, *refs):
    refs = list(refs)
    flags_ref = None if row_of is None else refs.pop(0)
    q_ref = refs.pop(0)
    state_in = [(refs.pop(0), refs.pop(0)) for _ in range(blocks_here)]
    arrived = [refs.pop(0) for _ in range(operands)]
    if last:
        out_hbm, out_ref, k_ref, vt_ref, sems = refs
    else:
        state_out = [(refs.pop(0), refs.pop(0)) for _ in range(blocks_here)]
        k_ref, vt_ref = refs
    me = lax.axis_index("ctx")
    origin = source(me)
    some = (origin >= 0) & (origin < me)
    per_block = q_ref.shape[0] // blocks_here // TILE
    tiles = per_block * blocks_here
    key_blocks = k_ref.shape[0] // BLOCK

    def finish(t, acc, highest, total):
        if not last:
            keep_state(*state_out[t // per_block], pl.ds(t % per_block * TILE, TILE), acc, highest, total)
            return
        rows = pl.ds(t * TILE, TILE)
        out_ref[rows, :] = (acc / total[:1]).astype(out_ref.dtype).T
        pltpu.make_async_copy(out_ref.at[rows], out_hbm.at[rows], sems.at[t]).start()

    @pl.when(some)
    def _():
        at = 0
        for ref in arrived:
            span = pl.ds(at, ref.shape[1])
            k_ref[span, :] = ref[0]
            vt_ref[:DH, span] = ref[1].T
            at += ref.shape[1]
        vt_ref[DH:, :] = jnp.ones((ONES, at), vt_ref.dtype)
        k, vt = k_ref[...], vt_ref[...]
        raw = scores(k, q_ref[pl.ds(0, TILE), :])
        for t in range(tiles):
            s = raw
            if t + 1 < tiles:
                raw = scores(k, q_ref[pl.ds((t + 1) * TILE, TILE), :])
            i, cols = t // per_block, pl.ds(t % per_block * TILE, TILE)
            acc_in, stat_in = state_in[i]
            before = stat_in[:1, cols]
            if row_of is None:
                highest = jnp.maximum(before, top_of(s))
                w = weights(s, highest * EXP2_SCALE)
            else:
                parts = [s[j * BLOCK : (j + 1) * BLOCK] for j in range(key_blocks)]
                at = [row_of + j * blocks_here + i for j in range(key_blocks)]
                off = [flags_ref[n : n + 1, :] for n in at]
                highest = reduce(jnp.maximum, [top_of(part) - o for part, o in zip(parts, off)], before)
                scaled = highest * EXP2_SCALE
                w = jnp.concatenate([weights(part, scaled + o) for part, o in zip(parts, off)], axis=0)
            sums = jnp.dot(vt, w, preferred_element_type=jnp.float32)
            keep = jnp.exp2((before - highest) * EXP2_SCALE)
            finish(t, acc_in[:, cols] * keep + sums[:DH], highest, stat_in[8:, cols] * keep + sums[DH : DH + 8])

    @pl.when(jnp.logical_not(some))
    def _():
        for t in range(tiles):
            cols = pl.ds(t % per_block * TILE, TILE)
            acc_in, stat_in = state_in[t // per_block]
            finish(t, acc_in[:, cols], stat_in[:1, cols], stat_in[8:, cols])

    if last:
        for t in range(tiles):
            rows = pl.ds(t * TILE, TILE)
            pltpu.make_async_copy(out_ref.at[rows], out_hbm.at[rows], sems.at[t]).wait()


VMEM_SPEC = pl.BlockSpec(memory_space=pltpu.VMEM)
SMEM_SPEC = pl.BlockSpec(memory_space=pltpu.SMEM)
ANY_SPEC = pl.BlockSpec(memory_space=pl.ANY)
PARAMS = pltpu.CompilerParams(vmem_limit_bytes=16 << 20)


def state_shapes(rows):
    return [jax.ShapeDtypeStruct((DH, rows), jnp.float32), jax.ShapeDtypeStruct((16, rows), jnp.float32)]


def cost(rows, keys):
    return pl.CostEstimate(flops=4 * rows * keys * DH, bytes_accessed=8 * rows * DH, transcendentals=rows * keys)


def call_local(i, q, parts, table, per_head):
    tokens = sum(a.shape[1] for a in parts)
    rows = BLOCK * per_head
    needs_table = i > 1
    return pl.pallas_call(
        functools.partial(local_stage, i, per_head, len(parts)),
        in_specs=[VMEM_SPEC] * (1 + len(parts)) + [SMEM_SPEC] * needs_table,
        out_specs=[VMEM_SPEC] * 2,
        out_shape=state_shapes(rows),
        scratch_shapes=[
            pltpu.VMEM((tokens, DH), q.dtype),
            pltpu.VMEM((tokens, DH), q.dtype),
            pltpu.VMEM((DH + ONES, (i + 1) * BLOCK), q.dtype),
        ],
        cost_estimate=cost(rows, (i + 1) * BLOCK),
        compiler_params=PARAMS,
    )(*([q, *parts] + [table] * needs_table))


def call_flags(stages, table, blocks_here):
    entries = sum(count for pieces in stages for _, _, count in pieces) * blocks_here
    return pl.pallas_call(
        functools.partial(flags_stage, stages, blocks_here),
        in_specs=[SMEM_SPEC],
        out_specs=VMEM_SPEC,
        out_shape=jax.ShapeDtypeStruct((-(-entries // 8) * 8, TILE), jnp.float32),
        compiler_params=PARAMS,
        name="flags",
    )(table)


def call_arrival(source, row_of, arrays, flags, q, state, last=False):
    rows = q.shape[0]
    keys = sum(a.shape[1] for a in arrays)
    scratch = [pltpu.VMEM((keys, DH), q.dtype), pltpu.VMEM((DH + ONES, keys), q.dtype)]
    if last:
        scratch = [pltpu.VMEM(q.shape, q.dtype), *scratch, pltpu.SemaphoreType.DMA((rows // TILE,))]
    args = [] if row_of is None else [flags]
    args += [q, *[a for pair in state for a in pair], *arrays]
    out = pl.pallas_call(
        functools.partial(arrival_stage, source, row_of, len(arrays), len(state), last),
        in_specs=[VMEM_SPEC] * len(args),
        out_specs=ANY_SPEC if last else [VMEM_SPEC] * (2 * len(state)),
        out_shape=jax.ShapeDtypeStruct(q.shape, q.dtype) if last else state_shapes(rows // len(state)) * len(state),
        scratch_shapes=scratch,
        cost_estimate=cost(rows, keys),
        compiler_params=PARAMS,
    )(*args)
    return out if last else [(out[2 * i], out[2 * i + 1]) for i in range(len(state))]


def shards(queries, key_states, value_states, block_table):
    tokens = queries.shape[0]
    per_head = queries.shape[2]
    blocks_here = tokens // BLOCK
    context_count = lax.axis_size("ctx")
    cores = lax.axis_size("qsub")
    per_core = blocks_here // cores
    core = lax.axis_index("qsub")
    q = queries.reshape(tokens * per_head, DH)
    k = key_states.reshape(tokens, DH)
    v = value_states.reshape(tokens, DH)

    part = per_core * BLOCK
    packed = jnp.stack(
        [lax.dynamic_slice_in_dim(k, core * part, part), lax.dynamic_slice_in_dim(v, core * part, part)]
    )

    def swapped(arrived):
        return [
            lax.ppermute(arrived, "qsub", [(c, (c + shift) % cores) for c in range(cores)])
            for shift in range(1, cores)
        ]

    def hop(block, route):
        return lax.ppermute(block, "ctx", route)

    def local(i, parts):
        return call_local(i, q, parts, block_table, per_head)

    def pieces_of(kind, source):
        pieces = []
        for shift in range(cores):
            base = lambda me, core, shift=shift: jnp.where(
                source(me) < 0, -1, source(me) * blocks_here + lax.rem(core - shift + cores, cores) * per_core
            )
            pieces.append((kind, base, per_core))
        return pieces

    def flags_of(stages):
        return call_flags(stages, block_table, blocks_here)

    if context_count == 4:
        ring = [0, 1, 3, 2]
        after = {d: ring[(ring.index(d) + 1) % 4] for d in ring}
        before = {d: ring[(ring.index(d) - 1) % 4] for d in ring}
        forward = [(d, after[d]) for d in range(4)]
        backward = [(d, before[d]) for d in range(4)]
        origins = [after, before, {d: after[after[d]] for d in range(4)}]
        sources = [
            lambda me, pairs=pairs: reduce(lambda acc, d: jnp.where(me == d, pairs[d], acc), range(4), jnp.int32(0))
            for pairs in origins
        ]
        tabled = [any(o < d and (o + 1) * blocks_here > SINKS for d, o in pairs.items()) for pairs in origins]
        row_of, listed = [], []
        for n in range(3):
            row_of.append(len(listed) * per_core * cores * blocks_here if tabled[n] else None)
            if tabled[n]:
                listed.append(pieces_of("all", sources[n]))

        one = hop(packed, backward)
        parts = [packed, *swapped(packed)]
        state = [local(0, parts)]
        held, state[0] = lax.optimization_barrier((packed, state[0]))
        other = hop(held, forward)
        flags = flags_of(listed) if listed else None
        state += [local(i, parts) for i in range(1, blocks_here)]
        one, state = lax.optimization_barrier((one, state))
        swap = swapped(one)
        two = hop(one, backward)
        state = call_arrival(sources[0], row_of[0], [one, *swap], flags, q, state)
        for n, arrived in ((1, other), (2, two)):
            arrived, state = lax.optimization_barrier((arrived, state))
            swap = swapped(arrived)
            row = row_of[n]
            state = call_arrival(sources[n], row, [arrived], flags, q, state)
            row = None if row is None else row + per_core * blocks_here
            state = call_arrival(sources[n], row, swap, flags, q, state, last=n == 2)
        attended = state
    else:
        parts = [packed, *swapped(packed)]
        state = [local(i, parts) for i in range(blocks_here)]
        wanted = []
        for level in range(LEVELS):
            amount = max(2**level // blocks_here, 1)
            if amount < context_count and amount not in wanted:
                wanted.append(amount)
        roots = -(-SINKS // blocks_here)
        position = lax.axis_index("ctx")
        shared = [
            lax.psum(jnp.where(position == root, packed, jnp.zeros_like(packed)), "ctx") for root in range(roots)
        ]
        stages = []
        moved, reached = packed, 0
        for amount in wanted:
            step = amount - reached
            moved = hop(moved, [(d, d + step) for d in range(context_count - step)])
            reached = amount
            stages.append((moved, "level", lambda me, amount=amount: jnp.maximum(me - amount, -1)))
        for root, arrived in enumerate(shared):
            stages.append((arrived, "sink", lambda me, root=root: jnp.int32(root)))
        flags = flags_of([pieces_of(kind, source) for _, kind, source in stages])
        for n, (arrived, _, source) in enumerate(stages):
            row = n * per_core * cores * blocks_here
            arrays = [arrived, *swapped(arrived)]
            state = call_arrival(source, row, arrays, flags, q, state, last=n == len(stages) - 1)
        attended = state
    return attended.reshape(tokens, 1, per_head, DH)


def solution(mesh):
    placed = (
        P(("groups", "ctx"), "head", "qsub", None),
        P(("groups", "ctx"), "head", None),
        P(("groups", "ctx"), "head", None),
        P(("groups", "ctx"), None),
    )

    return jax.shard_map(
        shards,
        mesh=mesh,
        in_specs=placed,
        out_specs=P(("groups", "ctx"), "head", "qsub", None),
        check_vma=False,
    )
```

time: 24.4 us -> 24.5 us (level)
  the two profiles are of different devices: /device:TPU:25 before, /device:TPU:0 now
where the time goes in v2:
time: 24.5 us; the launch traced here: 24.3 us
  waiting for transfers between devices  11.2 us (46%)
  starting transfers between devices  8.32 us (34%)
  Pallas kernels  3.73 us (15%)
  local copies, waits for them, and re-layouts  0.95 us (4%)
    ppermute x3, waiting for transfers between devices, hop(): return lax.ppermute(block, 'ctx', route)  9.9 us
    ppermute x3, starting transfers between devices, hop(): return lax.ppermute(block, 'ctx', route)  7.75 us
    pallas_call x2, Pallas kernels, call_local(): pl.pallas_call(functools.partial(local_stage, i, per_head, len(parts)), i...  1.87 us
    ppermute x4, waiting for transfers between devices, swapped(): lax.ppermute(arrived, 'qsub', [(c, (c + shift) % cores) for c in range(co...  1.27 us
    pallas_call x5, Pallas kernels, call_arrival(): pl.pallas_call(functools.partial(arrival_stage, source, row_of, len(array...  1.26 us
    another operation x1, local copies, waits for them, and re-layouts, shards(): jnp.stack([lax.dynamic_slice_in_dim(k, core * part, part), lax.dynamic_sl...  0.94 us
    pallas_call x1, Pallas kernels, call_flags(): pl.pallas_call(functools.partial(flags_stage, stages, blocks_here), in_sp...  0.6 us
    ppermute x4, starting transfers between devices, swapped(): lax.ppermute(arrived, 'qsub', [(c, (c + shift) % cores) for c in range(co...  0.57 us
  transfers between devices with their start and end apart: 7, of which 4 were waited for; matrix products, arithmetic and copies ran while one was open for 0% of the time, Pallas kernels for 12%

profile of v2, /device:TPU:0, one launch (start us, length us, event | category | flops | bytes accessed | tf_op | source)
XLA Modules:
  0.0 24.3 jit_solution(10779525965983294692)
XLA Ops:
  0.0 0.9 %dynamic-slice_bitcast_fusion = (bf16[1,256,128]{2,1,0:T(8,128)(2,1)S(1)}, bf16[1,256,128]{2,1,0:T(8,128)(2,1)S(1)}) fusion(bf16[512,1,128]{2,0,1:T(8,128)(2,1)} %param.6, s32[]{:T(128)S(6)} %select_n.4, bf16[512,1,128]{2,0,1:T(8,128)(2,1)} %param.5), kind=kLoop, calls=%fused_computation.1 | loop fusion | bytes 262148 | tf_op jit(solution)/shard_map/stack | solution.py:258
  1.0 0.6 %collective-permute-start.1 = (bf16[2,256,128]{2,1,0:T(8,128)(2,1)S(1)}, bf16[2,256,128]{2,1,0:T(8,128)(2,1)S(1)}, u32[]{:S(2)}, u32[]{:S(2)}) collective-permute-start(bf16[2,256,128]{2,1,0:T(8,128)(2,1)S(1)} %pad_maximum_fusion.refs_0_), channel_id=1, source_target_pairs={{0,1},{1,0},{2,3},{3,2},{4,5},{5,4},{6,7},{7,6},{8,9},{9,8},{10,11... | collective-permute-start | bytes 393224 | tf_op jit(solution)/shard_map/ppermute | solution.py:264
  1.5 3.6 %collective-permute-start = (bf16[2,256,128]{2,1,0:T(8,128)(2,1)S(1)}, bf16[2,256,128]{2,1,0:T(8,128)(2,1)S(1)}, u32[]{:S(2)}, u32[]{:S(2)}) collective-permute-start(bf16[2,256,128]{2,1,0:T(8,128)(2,1)S(1)} %pad_maximum_fusion.refs_0_), channel_id=1, source_target_pairs={{0,8},{4,0},{8,12},{12,4},{1,9},{5,1},{9,13},{13,5},{2,10},{6,2},{... | collective-permute-start | bytes 393224 | tf_op jit(solution)/shard_map/ppermute | solution.py:269
  5.2 0.0 collective-permute-done.1.refs_1_
  5.2 0.7 %shard_map.46 = (f32[128,1024]{1,0:T(8,128)S(1)}, f32[16,1024]{1,0:T(8,128)S(1)}) custom-call(bf16[2048,128]{1,0:T(8,128)(2,1)S(1)} %bitcast.8, bf16[2,256,128]{2,1,0:T(8,128)(2,1)S(1)} %pad_maximum_fusion.refs_0_, bf16[2,256,128]{2,1,0:T(8,128)(2,1)S(1)} %collective-permute-done.1.refs_1_), custom_call_target="tpu_custom_call" | custom-call | flops 134217728 | bytes 1048576 | tf_op jit(solution)/shard_map/pallas_call | solution.py:198
  5.9 1.1 %shard_map.47 = (f32[128,1024]{1,0:T(8,128)S(1)}, f32[16,1024]{1,0:T(8,128)S(1)}) custom-call(bf16[2048,128]{1,0:T(8,128)(2,1)S(1)} %bitcast.9, bf16[2,256,128]{2,1,0:T(8,128)(2,1)S(1)} %pad_maximum_fusion.refs_0_, bf16[2,256,128]{2,1,0:T(8,128)(2,1)S(1)} %collective-permute-done.1.refs_1_), custom_call_target="tpu_custom_call" | custom-call | flops 268435456 | bytes 1048576 | tf_op jit(solution)/shard_map/pallas_call | solution.py:198
  7.0 1.5 %collective-permute-done.refs_6_ = bf16[2,256,128]{2,1,0:T(8,128)(2,1)S(1)} collective-permute-done((bf16[2,256,128]{2,1,0:T(8,128)(2,1)S(1)}, bf16[2,256,128]{2,1,0:T(8,128)(2,1)S(1)}, u32[]{:S(2)}, u32[]{:S(2)}) %collective-permute-start) | collective-permute-done | bytes 131104 | tf_op jit(solution)/shard_map/ppermute | solution.py:269
  8.5 0.0 collective-permute-start.4
  8.5 2.4 %collective-permute-start.3 = (bf16[2,256,128]{2,1,0:T(8,128)(2,1)S(1)}, bf16[2,256,128]{2,1,0:T(8,128)(2,1)S(1)}, u32[]{:S(2)}, u32[]{:S(2)}) collective-permute-start(bf16[2,256,128]{2,1,0:T(8,128)(2,1)S(1)} %pad_maximum_fusion.refs_0_), channel_id=1, source_target_pairs={{0,4},{4,12},{8,0},{12,8},{1,5},{5,13},{9,1},{13,9},{2,6},{6,14},{... | collective-permute-start | bytes 393224 | tf_op jit(solution)/shard_map/ppermute | solution.py:269
  10.9 0.0 copy-done.1
  10.9 0.6 %flags.1.refs_0_ = f32[8,512]{1,0:T(8,128)S(1)} custom-call(s32[2,7]{1,0:T(2,128)S(1)} %copy-done.1), custom_call_target="tpu_custom_call" | custom-call | tf_op jit(solution)/shard_map/flags/pallas_call | solution.py:215
  11.5 0.0 collective-permute-done.4.refs_7_
  11.5 0.1 shard_map.48
  11.6 4.5 %collective-permute-done.3.refs_5_ = bf16[2,256,128]{2,1,0:T(8,128)(2,1)S(1)} collective-permute-done((bf16[2,256,128]{2,1,0:T(8,128)(2,1)S(1)}, bf16[2,256,128]{2,1,0:T(8,128)(2,1)S(1)}, u32[]{:S(2)}, u32[]{:S(2)}) %collective-permute-start.3) | collective-permute-done | bytes 131104 | tf_op jit(solution)/shard_map/ppermute | solution.py:269
  16.1 0.0 collective-permute-start.5
  16.1 1.7 %collective-permute-start.2 = (bf16[2,256,128]{2,1,0:T(8,128)(2,1)S(1)}, bf16[2,256,128]{2,1,0:T(8,128)(2,1)S(1)}, u32[]{:S(2)}, u32[]{:S(2)}) collective-permute-start(bf16[2,256,128]{2,1,0:T(8,128)(2,1)S(1)} %collective-permute-done.refs_6_), channel_id=1, source_target_pairs={{0,8},{4,0},{8,12},{12,4},{1,9},{5,1},{9,13},{13,5},{2,10},{6,2},{... | collective-permute-start | bytes 393224 | tf_op jit(solution)/shard_map/ppermute | solution.py:269
  17.8 0.1 shard_map.49
  17.9 0.0 collective-permute-done.5.refs_5_
  17.9 0.1 shard_map.50
  18.0 4.0 %collective-permute-done.2.refs_5_ = bf16[2,256,128]{2,1,0:T(8,128)(2,1)S(1)} collective-permute-done((bf16[2,256,128]{2,1,0:T(8,128)(2,1)S(1)}, bf16[2,256,128]{2,1,0:T(8,128)(2,1)S(1)}, u32[]{:S(2)}, u32[]{:S(2)}) %collective-permute-start.2) | collective-permute-done | bytes 131104 | tf_op jit(solution)/shard_map/ppermute | solution.py:269
  22.0 0.0 collective-permute-start.6
  22.0 0.1 shard_map.51
  22.1 1.3 %collective-permute-done.6.refs_5_ = bf16[2,256,128]{2,1,0:T(8,128)(2,1)S(1)} collective-permute-done((bf16[2,256,128]{2,1,0:T(8,128)(2,1)S(1)}, bf16[2,256,128]{2,1,0:T(8,128)(2,1)S(1)}, u32[]{:S(2)}, u32[]{:S(2)}) %collective-permute-start.6) | collective-permute-done | bytes 131104 | tf_op jit(solution)/shard_map/ppermute | solution.py:264
  23.3 0.9 %shard_map.52 = bf16[2048,128]{1,0:T(8,128)(2,1)} custom-call(bf16[2048,128]{1,0:T(8,128)(2,1)S(1)} %bitcast.14, f32[128,1024]{1,0:T(8,128)S(1)} %get-tuple-element.77.refs_1_, f32[16,1024]{1,0:T(8,128)S(1)} %get-tuple-element.78.refs_2_, f32[128,1024]{1,0:T(8,128)S(1)} %get-tuple-element.79.refs_3_, f32[16,1024]{1,0:T(8,128)S(1)} %get-tuple-element.80.refs_4_, ...), custom_call_target="tpu_custom_call" | custom-call | flops 268435456 | bytes 2097152 | tf_op jit(solution)/shard_map/pallas_call | solution.py:233
  (4 shorter events, 0.0 us)
Async XLA Ops:
  0.0 5.2 %copy-start = (bf16[512,1,4,128]{3,2,1,0:T(4,128)(2,1)S(1)}, bf16[512,1,4,128]{3,2,1,0:T(4,128)(2,1)}, u32[]{:S(2)}) copy-start(bf16[512,1,4,128]{3,2,1,0:T(4,128)(2,1)} %param.4) | copy-start | bytes 1572868
  1.0 4.2 %collective-permute-start.1 = (bf16[2,256,128]{2,1,0:T(8,128)(2,1)S(1)}, bf16[2,256,128]{2,1,0:T(8,128)(2,1)S(1)}, u32[]{:S(2)}, u32[]{:S(2)}) collective-permute-start(bf16[2,256,128]{2,1,0:T(8,128)(2,1)S(1)} %pad_maximum_fusion.refs_0_), channel_id=1, source_target_pairs={{0,1},{1,0},{2,3},{3,2},{4,5},{5,4},{6,7},{7,6},{8,9},{9,8},{10,11... | collective-permute-start | bytes 393224 | tf_op jit(solution)/shard_map/ppermute | solution.py:264
  1.5 7.0 %collective-permute-start = (bf16[2,256,128]{2,1,0:T(8,128)(2,1)S(1)}, bf16[2,256,128]{2,1,0:T(8,128)(2,1)S(1)}, u32[]{:S(2)}, u32[]{:S(2)}) collective-permute-start(bf16[2,256,128]{2,1,0:T(8,128)(2,1)S(1)} %pad_maximum_fusion.refs_0_), channel_id=1, source_target_pairs={{0,8},{4,0},{8,12},{12,4},{1,9},{5,1},{9,13},{13,5},{2,10},{6,2},{... | collective-permute-start | bytes 393224 | tf_op jit(solution)/shard_map/ppermute | solution.py:269
  8.5 2.4 %copy-start.1 = (s32[2,7]{1,0:T(2,128)S(1)}, s32[2,7]{1,0:T(2,128)}, u32[]{:S(2)}) copy-start(s32[2,7]{1,0:T(2,128)} %table_ref.1) | copy-start | bytes 172
  8.5 3.0 %collective-permute-start.4 = (bf16[2,256,128]{2,1,0:T(8,128)(2,1)S(1)}, bf16[2,256,128]{2,1,0:T(8,128)(2,1)S(1)}, u32[]{:S(2)}, u32[]{:S(2)}) collective-permute-start(bf16[2,256,128]{2,1,0:T(8,128)(2,1)S(1)} %collective-permute-done.refs_6_), channel_id=1, source_target_pairs={{0,1},{1,0},{2,3},{3,2},{4,5},{5,4},{6,7},{7,6},{8,9},{9,8},{10,11... | collective-permute-start | bytes 393224 | tf_op jit(solution)/shard_map/ppermute | solution.py:264
  8.5 7.5 %collective-permute-start.3 = (bf16[2,256,128]{2,1,0:T(8,128)(2,1)S(1)}, bf16[2,256,128]{2,1,0:T(8,128)(2,1)S(1)}, u32[]{:S(2)}, u32[]{:S(2)}) collective-permute-start(bf16[2,256,128]{2,1,0:T(8,128)(2,1)S(1)} %pad_maximum_fusion.refs_0_), channel_id=1, source_target_pairs={{0,4},{4,12},{8,0},{12,8},{1,5},{5,13},{9,1},{13,9},{2,6},{6,14},{... | collective-permute-start | bytes 393224 | tf_op jit(solution)/shard_map/ppermute | solution.py:269
  16.1 1.8 %collective-permute-start.5 = (bf16[2,256,128]{2,1,0:T(8,128)(2,1)S(1)}, bf16[2,256,128]{2,1,0:T(8,128)(2,1)S(1)}, u32[]{:S(2)}, u32[]{:S(2)}) collective-permute-start(bf16[2,256,128]{2,1,0:T(8,128)(2,1)S(1)} %collective-permute-done.3.refs_5_), channel_id=1, source_target_pairs={{0,1},{1,0},{2,3},{3,2},{4,5},{5,4},{6,7},{7,6},{8,9},{9,8},{10,11... | collective-permute-start | bytes 393224 | tf_op jit(solution)/shard_map/ppermute | solution.py:264
  16.1 5.9 %collective-permute-start.2 = (bf16[2,256,128]{2,1,0:T(8,128)(2,1)S(1)}, bf16[2,256,128]{2,1,0:T(8,128)(2,1)S(1)}, u32[]{:S(2)}, u32[]{:S(2)}) collective-permute-start(bf16[2,256,128]{2,1,0:T(8,128)(2,1)S(1)} %collective-permute-done.refs_6_), channel_id=1, source_target_pairs={{0,8},{4,0},{8,12},{12,4},{1,9},{5,1},{9,13},{13,5},{2,10},{6,2},{... | collective-permute-start | bytes 393224 | tf_op jit(solution)/shard_map/ppermute | solution.py:269
  22.0 1.3 %collective-permute-start.6 = (bf16[2,256,128]{2,1,0:T(8,128)(2,1)S(1)}, bf16[2,256,128]{2,1,0:T(8,128)(2,1)S(1)}, u32[]{:S(2)}, u32[]{:S(2)}) collective-permute-start(bf16[2,256,128]{2,1,0:T(8,128)(2,1)S(1)} %collective-permute-done.2.refs_5_), channel_id=1, source_target_pairs={{0,1},{1,0},{2,3},{3,2},{4,5},{5,4},{6,7},{7,6},{8,9},{9,8},{10,11... | collective-permute-start | bytes 393224 | tf_op jit(solution)/shard_map/ppermute | solution.py:264

commit v3 on v2

--- a/solution.py
+++ b/solution.py
@@ -129,7 +129,7 @@
             keep_state(*state_out[t // per_block], pl.ds(t % per_block * TILE, TILE), acc, highest, total)
             return
         rows = pl.ds(t * TILE, TILE)
-        out_ref[rows, :] = (acc / total[:1]).astype(out_ref.dtype).T
+        out_ref[rows, :] = (acc * (1.0 / total[:1])).astype(out_ref.dtype).T
         pltpu.make_async_copy(out_ref.at[rows], out_hbm.at[rows], sems.at[t]).start()
 
     @pl.when(some)
@@ -284,12 +284,12 @@
         return call_flags(stages, block_table, blocks_here)
 
     if context_count == 4:
-        ring = [0, 1, 3, 2]
+        ring = [0, 1, 2, 3]
         after = {d: ring[(ring.index(d) + 1) % 4] for d in ring}
         before = {d: ring[(ring.index(d) - 1) % 4] for d in ring}
         forward = [(d, after[d]) for d in range(4)]
         backward = [(d, before[d]) for d in range(4)]
-        origins = [after, before, {d: after[after[d]] for d in range(4)}]
+        origins = [before, after, {0: 3, 1: 2, 2: 0, 3: 1}]
         sources = [
             lambda me, pairs=pairs: reduce(lambda acc, d: jnp.where(me == d, pairs[d], acc), range(4), jnp.int32(0))
             for pairs in origins
@@ -301,16 +301,18 @@
             if tabled[n]:
                 listed.append(pieces_of("all", sources[n]))
 
-        one = hop(packed, backward)
+        one = hop(packed, forward)
         parts = [packed, *swapped(packed)]
         state = [local(0, parts)]
         held, state[0] = lax.optimization_barrier((packed, state[0]))
-        other = hop(held, forward)
+        other = hop(held, backward)
         flags = flags_of(listed) if listed else None
         state += [local(i, parts) for i in range(1, blocks_here)]
         one, state = lax.optimization_barrier((one, state))
         swap = swapped(one)
-        two = hop(one, backward)
+        route = [(c, (c + 1) % cores) for c in range(cores)]
+        route += [(a * cores + c, b * cores + c) for a, b in ((1, 2), (2, 3), (3, 1)) for c in range(cores)]
+        two = lax.ppermute(one, ("ctx", "qsub"), route)
         state = call_arrival(sources[0], row_of[0], [one, *swap], flags, q, state)
         for n, arrived in ((1, other), (2, two)):
             arrived, state = lax.optimization_barrier((arrived, state))

time: 24.5 us -> 24.5 us (level)
  the two profiles are of different devices: /device:TPU:0 before, /device:TPU:31 now
where the time goes in v3:
time: 24.5 us; the launch traced here: 24.4 us
  waiting for transfers between devices  9.97 us (41%)
  Pallas kernels  9.78 us (40%)
  starting transfers between devices  3.56 us (15%)
  local copies, waits for them, and re-layouts  0.95 us (4%)
    pallas_call x5, Pallas kernels, call_arrival(): pl.pallas_call(functools.partial(arrival_stage, source, row_of, len(array...  7.32 us
    ppermute x2, waiting for transfers between devices, hop(): return lax.ppermute(block, 'ctx', route)  6 us
    ppermute x4, starting transfers between devices, swapped(): lax.ppermute(arrived, 'qsub', [(c, (c + shift) % cores) for c in range(co...  3.38 us
    ppermute x1, waiting for transfers between devices, shards(): two = lax.ppermute(one, ('ctx', 'qsub'), route)  2.77 us
    pallas_call x2, Pallas kernels, call_local(): pl.pallas_call(functools.partial(local_stage, i, per_head, len(parts)), i...  1.87 us
    ppermute x4, waiting for transfers between devices, swapped(): lax.ppermute(arrived, 'qsub', [(c, (c + shift) % cores) for c in range(co...  1.2 us
    another operation x1, local copies, waits for them, and re-layouts, shards(): jnp.stack([lax.dynamic_slice_in_dim(k, core * part, part), lax.dynamic_sl...  0.94 us
    pallas_call x1, Pallas kernels, call_flags(): pl.pallas_call(functools.partial(flags_stage, stages, blocks_here), in_sp...  0.6 us
  transfers between devices with their start and end apart: 7, of which 5 were waited for; matrix products, arithmetic and copies ran while one was open for 0% of the time, Pallas kernels for 32%

profile of v3, /device:TPU:31, one launch (start us, length us, event | category | flops | bytes accessed | tf_op | source)
XLA Modules:
  0.0 24.4 jit_solution(8550003816909369680)
XLA Ops:
  0.0 0.9 %dynamic-slice_bitcast_fusion = (bf16[1,256,128]{2,1,0:T(8,128)(2,1)S(1)}, bf16[1,256,128]{2,1,0:T(8,128)(2,1)S(1)}) fusion(bf16[512,1,128]{2,0,1:T(8,128)(2,1)} %param.6, s32[]{:T(128)S(6)} %select_n.4, bf16[512,1,128]{2,0,1:T(8,128)(2,1)} %param.5), kind=kLoop, calls=%fused_computation.1 | loop fusion | bytes 262148 | tf_op jit(solution)/shard_map/stack | solution.py:258
  1.0 0.7 %collective-permute-start.1 = (bf16[2,256,128]{2,1,0:T(8,128)(2,1)S(1)}, bf16[2,256,128]{2,1,0:T(8,128)(2,1)S(1)}, u32[]{:S(2)}, u32[]{:S(2)}) collective-permute-start(bf16[2,256,128]{2,1,0:T(8,128)(2,1)S(1)} %pad_maximum_fusion.refs_0_), channel_id=1, source_target_pairs={{0,1},{1,0},{2,3},{3,2},{4,5},{5,4},{6,7},{7,6},{8,9},{9,8},{10,11... | collective-permute-start | bytes 393224 | tf_op jit(solution)/shard_map/ppermute | solution.py:264
  1.7 0.0 collective-permute-start
  1.7 1.0 %collective-permute-done.1.refs_1_ = bf16[2,256,128]{2,1,0:T(8,128)(2,1)S(1)} collective-permute-done((bf16[2,256,128]{2,1,0:T(8,128)(2,1)S(1)}, bf16[2,256,128]{2,1,0:T(8,128)(2,1)S(1)}, u32[]{:S(2)}, u32[]{:S(2)}) %collective-permute-start.1) | collective-permute-done | bytes 131104 | tf_op jit(solution)/shard_map/ppermute | solution.py:264
  2.7 0.0 copy-done
  2.7 0.7 %shard_map.46 = (f32[128,1024]{1,0:T(8,128)S(1)}, f32[16,1024]{1,0:T(8,128)S(1)}) custom-call(bf16[2048,128]{1,0:T(8,128)(2,1)S(1)} %bitcast.8, bf16[2,256,128]{2,1,0:T(8,128)(2,1)S(1)} %pad_maximum_fusion.refs_0_, bf16[2,256,128]{2,1,0:T(8,128)(2,1)S(1)} %collective-permute-done.1.refs_1_), custom_call_target="tpu_custom_call" | custom-call | flops 134217728 | bytes 1048576 | tf_op jit(solution)/shard_map/pallas_call | solution.py:198
  3.4 1.1 %shard_map.47 = (f32[128,1024]{1,0:T(8,128)S(1)}, f32[16,1024]{1,0:T(8,128)S(1)}) custom-call(bf16[2048,128]{1,0:T(8,128)(2,1)S(1)} %bitcast.9, bf16[2,256,128]{2,1,0:T(8,128)(2,1)S(1)} %pad_maximum_fusion.refs_0_, bf16[2,256,128]{2,1,0:T(8,128)(2,1)S(1)} %collective-permute-done.1.refs_1_), custom_call_target="tpu_custom_call" | custom-call | flops 268435456 | bytes 1048576 | tf_op jit(solution)/shard_map/pallas_call | solution.py:198
  4.6 2.1 %collective-permute-done.refs_6_ = bf16[2,256,128]{2,1,0:T(8,128)(2,1)S(1)} collective-permute-done((bf16[2,256,128]{2,1,0:T(8,128)(2,1)S(1)}, bf16[2,256,128]{2,1,0:T(8,128)(2,1)S(1)}, u32[]{:S(2)}, u32[]{:S(2)}) %collective-permute-start) | collective-permute-done | bytes 131104 | tf_op jit(solution)/shard_map/ppermute | solution.py:269
  6.7 0.9 %collective-permute-start.4 = (bf16[2,256,128]{2,1,0:T(8,128)(2,1)S(1)}, bf16[2,256,128]{2,1,0:T(8,128)(2,1)S(1)}, u32[]{:S(2)}, u32[]{:S(2)}) collective-permute-start(bf16[2,256,128]{2,1,0:T(8,128)(2,1)S(1)} %collective-permute-done.refs_6_), channel_id=1, source_target_pairs={{0,1},{1,0},{2,3},{3,2},{4,5},{5,4},{6,7},{7,6},{8,9},{9,8},{10,11... | collective-permute-start | bytes 393224 | tf_op jit(solution)/shard_map/ppermute | solution.py:264
  7.6 0.2 collective-permute-start.3
  7.8 0.6 %flags.1.refs_0_ = f32[8,512]{1,0:T(8,128)S(1)} custom-call(s32[2,7]{1,0:T(2,128)S(1)} %copy-done.1), custom_call_target="tpu_custom_call" | custom-call | tf_op jit(solution)/shard_map/flags/pallas_call | solution.py:215
  8.4 0.2 collective-permute-done.4.refs_7_
  8.6 2.0 %shard_map.48 = (f32[128,1024]{1,0:T(8,128)S(1)}, f32[16,1024]{1,0:T(8,128)S(1)}, f32[128,1024]{1,0:T(8,128)S(1)}, f32[16,1024]{1,0:T(8,128)S(1)}) custom-call(f32[8,512]{1,0:T(8,128)S(1)} %flags.1.refs_0_, bf16[2048,128]{1,0:T(8,128)(2,1)S(1)} %bitcast.10, f32[128,1024]{1,0:T(8,128)S(1)} %get-tuple-element.51.refs_2_, ...), custom_call_target="tpu_custom_call" | custom-call | flops 536870912 | bytes 2097152 | tf_op jit(solution)/shard_map/pallas_call | solution.py:233
  10.6 3.9 %collective-permute-done.3.refs_5_ = bf16[2,256,128]{2,1,0:T(8,128)(2,1)S(1)} collective-permute-done((bf16[2,256,128]{2,1,0:T(8,128)(2,1)S(1)}, bf16[2,256,128]{2,1,0:T(8,128)(2,1)S(1)}, u32[]{:S(2)}, u32[]{:S(2)}) %collective-permute-start.3) | collective-permute-done | bytes 131104 | tf_op jit(solution)/shard_map/ppermute | solution.py:269
  14.5 0.9 %collective-permute-start.5 = (bf16[2,256,128]{2,1,0:T(8,128)(2,1)S(1)}, bf16[2,256,128]{2,1,0:T(8,128)(2,1)S(1)}, u32[]{:S(2)}, u32[]{:S(2)}) collective-permute-start(bf16[2,256,128]{2,1,0:T(8,128)(2,1)S(1)} %collective-permute-done.3.refs_5_), channel_id=1, source_target_pairs={{0,1},{1,0},{2,3},{3,2},{4,5},{5,4},{6,7},{7,6},{8,9},{9,8},{10,11... | collective-permute-start | bytes 393224 | tf_op jit(solution)/shard_map/ppermute | solution.py:264
  15.3 0.0 collective-permute-start.2
  15.3 1.1 %shard_map.49 = (f32[128,1024]{1,0:T(8,128)S(1)}, f32[16,1024]{1,0:T(8,128)S(1)}, f32[128,1024]{1,0:T(8,128)S(1)}, f32[16,1024]{1,0:T(8,128)S(1)}) custom-call(bf16[2048,128]{1,0:T(8,128)(2,1)S(1)} %bitcast.11, f32[128,1024]{1,0:T(8,128)S(1)} %get-tuple-element.59.refs_1_, f32[16,1024]{1,0:T(8,128)S(1)} %get-tuple-element.60.refs_2_, ...), custom_call_target="tpu_custom_call" | custom-call | flops 268435456 | bytes 2097152 | tf_op jit(solution)/shard_map/pallas_call | solution.py:233
  16.5 0.0 collective-permute-done.5.refs_5_
  16.5 1.1 %shard_map.50 = (f32[128,1024]{1,0:T(8,128)S(1)}, f32[16,1024]{1,0:T(8,128)S(1)}, f32[128,1024]{1,0:T(8,128)S(1)}, f32[16,1024]{1,0:T(8,128)S(1)}) custom-call(bf16[2048,128]{1,0:T(8,128)(2,1)S(1)} %bitcast.12, f32[128,1024]{1,0:T(8,128)S(1)} %get-tuple-element.64.refs_1_, f32[16,1024]{1,0:T(8,128)S(1)} %get-tuple-element.65.refs_2_, ...), custom_call_target="tpu_custom_call" | custom-call | flops 268435456 | bytes 2097152 | tf_op jit(solution)/shard_map/pallas_call | solution.py:233
  17.6 2.8 %collective-permute-done.2.refs_5_ = bf16[2,256,128]{2,1,0:T(8,128)(2,1)S(1)} collective-permute-done((bf16[2,256,128]{2,1,0:T(8,128)(2,1)S(1)}, bf16[2,256,128]{2,1,0:T(8,128)(2,1)S(1)}, u32[]{:S(2)}, u32[]{:S(2)}) %collective-permute-start.2) | collective-permute-done | bytes 131104 | tf_op jit(solution)/shard_map/ppermute | solution.py:315
  20.4 0.9 %collective-permute-start.6 = (bf16[2,256,128]{2,1,0:T(8,128)(2,1)S(1)}, bf16[2,256,128]{2,1,0:T(8,128)(2,1)S(1)}, u32[]{:S(2)}, u32[]{:S(2)}) collective-permute-start(bf16[2,256,128]{2,1,0:T(8,128)(2,1)S(1)} %collective-permute-done.2.refs_5_), channel_id=1, source_target_pairs={{0,1},{1,0},{2,3},{3,2},{4,5},{5,4},{6,7},{7,6},{8,9},{9,8},{10,11... | collective-permute-start | bytes 393224 | tf_op jit(solution)/shard_map/ppermute | solution.py:264
  21.2 1.1 %shard_map.51 = (f32[128,1024]{1,0:T(8,128)S(1)}, f32[16,1024]{1,0:T(8,128)S(1)}, f32[128,1024]{1,0:T(8,128)S(1)}, f32[16,1024]{1,0:T(8,128)S(1)}) custom-call(bf16[2048,128]{1,0:T(8,128)(2,1)S(1)} %bitcast.13, f32[128,1024]{1,0:T(8,128)S(1)} %get-tuple-element.72.refs_1_, f32[16,1024]{1,0:T(8,128)S(1)} %get-tuple-element.73.refs_2_, ...), custom_call_target="tpu_custom_call" | custom-call | flops 268435456 | bytes 2097152 | tf_op jit(solution)/shard_map/pallas_call | solution.py:233
  22.4 0.0 collective-permute-done.6.refs_5_
  22.4 2.0 %shard_map.52 = bf16[2048,128]{1,0:T(8,128)(2,1)} custom-call(bf16[2048,128]{1,0:T(8,128)(2,1)S(1)} %bitcast.14, f32[128,1024]{1,0:T(8,128)S(1)} %get-tuple-element.77.refs_1_, f32[16,1024]{1,0:T(8,128)S(1)} %get-tuple-element.78.refs_2_, f32[128,1024]{1,0:T(8,128)S(1)} %get-tuple-element.79.refs_3_, f32[16,1024]{1,0:T(8,128)S(1)} %get-tuple-element.80.refs_4_, ...), custom_call_target="tpu_custom_call" | custom-call | flops 268435456 | bytes 2097152 | tf_op jit(solution)/shard_map/pallas_call | solution.py:233
  (4 shorter events, 0.0 us)
Async XLA Ops:
  0.0 2.7 %copy-start = (bf16[512,1,4,128]{3,2,1,0:T(4,128)(2,1)S(1)}, bf16[512,1,4,128]{3,2,1,0:T(4,128)(2,1)}, u32[]{:S(2)}) copy-start(bf16[512,1,4,128]{3,2,1,0:T(4,128)(2,1)} %param.4) | copy-start | bytes 1572868
  1.0 1.7 %collective-permute-start.1 = (bf16[2,256,128]{2,1,0:T(8,128)(2,1)S(1)}, bf16[2,256,128]{2,1,0:T(8,128)(2,1)S(1)}, u32[]{:S(2)}, u32[]{:S(2)}) collective-permute-start(bf16[2,256,128]{2,1,0:T(8,128)(2,1)S(1)} %pad_maximum_fusion.refs_0_), channel_id=1, source_target_pairs={{0,1},{1,0},{2,3},{3,2},{4,5},{5,4},{6,7},{7,6},{8,9},{9,8},{10,11... | collective-permute-start | bytes 393224 | tf_op jit(solution)/shard_map/ppermute | solution.py:264
  1.7 5.0 %collective-permute-start = (bf16[2,256,128]{2,1,0:T(8,128)(2,1)S(1)}, bf16[2,256,128]{2,1,0:T(8,128)(2,1)S(1)}, u32[]{:S(2)}, u32[]{:S(2)}) collective-permute-start(bf16[2,256,128]{2,1,0:T(8,128)(2,1)S(1)} %pad_maximum_fusion.refs_0_), channel_id=1, source_target_pairs={{0,4},{4,8},{8,12},{12,0},{1,5},{5,9},{9,13},{13,1},{2,6},{6,10},{... | collective-permute-start | bytes 393224 | tf_op jit(solution)/shard_map/ppermute | solution.py:269
  6.7 1.1 %copy-start.1 = (s32[2,7]{1,0:T(2,128)S(1)}, s32[2,7]{1,0:T(2,128)}, u32[]{:S(2)}) copy-start(s32[2,7]{1,0:T(2,128)} %table_ref.1) | copy-start | bytes 172
  6.7 1.9 %collective-permute-start.4 = (bf16[2,256,128]{2,1,0:T(8,128)(2,1)S(1)}, bf16[2,256,128]{2,1,0:T(8,128)(2,1)S(1)}, u32[]{:S(2)}, u32[]{:S(2)}) collective-permute-start(bf16[2,256,128]{2,1,0:T(8,128)(2,1)S(1)} %collective-permute-done.refs_6_), channel_id=1, source_target_pairs={{0,1},{1,0},{2,3},{3,2},{4,5},{5,4},{6,7},{7,6},{8,9},{9,8},{10,11... | collective-permute-start | bytes 393224 | tf_op jit(solution)/shard_map/ppermute | solution.py:264
  7.6 6.8 %collective-permute-start.3 = (bf16[2,256,128]{2,1,0:T(8,128)(2,1)S(1)}, bf16[2,256,128]{2,1,0:T(8,128)(2,1)S(1)}, u32[]{:S(2)}, u32[]{:S(2)}) collective-permute-start(bf16[2,256,128]{2,1,0:T(8,128)(2,1)S(1)} %pad_maximum_fusion.refs_0_), channel_id=1, source_target_pairs={{0,12},{4,0},{8,4},{12,8},{1,13},{5,1},{9,5},{13,9},{2,14},{6,2},{... | collective-permute-start | bytes 393224 | tf_op jit(solution)/shard_map/ppermute | solution.py:269
  14.5 2.0 %collective-permute-start.5 = (bf16[2,256,128]{2,1,0:T(8,128)(2,1)S(1)}, bf16[2,256,128]{2,1,0:T(8,128)(2,1)S(1)}, u32[]{:S(2)}, u32[]{:S(2)}) collective-permute-start(bf16[2,256,128]{2,1,0:T(8,128)(2,1)S(1)} %collective-permute-done.3.refs_5_), channel_id=1, source_target_pairs={{0,1},{1,0},{2,3},{3,2},{4,5},{5,4},{6,7},{7,6},{8,9},{9,8},{10,11... | collective-permute-start | bytes 393224 | tf_op jit(solution)/shard_map/ppermute | solution.py:264
  15.3 5.1 %collective-permute-start.2 = (bf16[2,256,128]{2,1,0:T(8,128)(2,1)S(1)}, bf16[2,256,128]{2,1,0:T(8,128)(2,1)S(1)}, u32[]{:S(2)}, u32[]{:S(2)}) collective-permute-start(bf16[2,256,128]{2,1,0:T(8,128)(2,1)S(1)} %collective-permute-done.refs_6_), channel_id=1, source_target_pairs={{0,1},{1,0},{4,8},{5,9},{8,12},{9,13},{12,4},{13,5},{2,3},{3,2},{6... | collective-permute-start | bytes 393224 | tf_op jit(solution)/shard_map/ppermute | solution.py:315
  20.4 2.0 %collective-permute-start.6 = (bf16[2,256,128]{2,1,0:T(8,128)(2,1)S(1)}, bf16[2,256,128]{2,1,0:T(8,128)(2,1)S(1)}, u32[]{:S(2)}, u32[]{:S(2)}) collective-permute-start(bf16[2,256,128]{2,1,0:T(8,128)(2,1)S(1)} %collective-permute-done.2.refs_5_), channel_id=1, source_target_pairs={{0,1},{1,0},{2,3},{3,2},{4,5},{5,4},{6,7},{7,6},{8,9},{9,8},{10,11... | collective-permute-start | bytes 393224 | tf_op jit(solution)/shard_map/ppermute | solution.py:264
